TPU v7x, 256 devices: a whole 4x4x8 slice. The times are simulated.
256 devices in a mesh: blk: 8 (over z), lat: 4 (over x), depth: 8 (over y, core).
Axes of the slice: x: 4, y: 4, z: 8, core: 2. Of those that a mesh axis runs over, the one named last changes fastest.
Arguments:
- face_len: int32 [8, 4, 8, 6], P('blk', 'lat', 'depth'), may hold values from 0 to 128, as said below
- residual: float32 [8, 4, 8, 768, 512], P('blk', 'lat', 'depth'), as said below
- prev_direction: float32 [8, 4, 8, 768, 512], P('blk', 'lat', 'depth'), as said below
- prev_rho: float32 [512], replicated, may hold values from 0.5 to 4
- schur: float32 [8, 4, 8, 768, 768], P('blk', 'lat', 'depth'), as said below
- neumann: float32 [8, 4, 8, 768, 768], P('blk', 'lat', 'depth'), as said below
- coarse_basis: float32 [8, 4, 8, 768, 256], P('blk', 'lat', 'depth'), may hold values from -0.21875 to 0.21875
- coarse_inverse: float32 [8, 4, 8, 256, 256], P('blk', 'lat', 'depth'), as said below
- prim_owner: int32 [8, 4, 8, 256, 1], P('blk', 'lat', 'depth'), may hold values from 0 to 31; in each aligned block of 256 rows (0 to 255, 256 to 511, ..., all dimensions but the last counted through in order) at most 24 rows name the same one
- coarse_row: int32 [8, 4, 8, 256], P('blk', 'lat', 'depth'), may hold values from 0 to 255
Outputs:
- new_residual: float32 [8, 4, 8, 768, 512], P('blk', 'lat', 'depth')
- direction: float32 [8, 4, 8, 768, 512], P('blk', 'lat', 'depth')
- rho_now: float32 [512], replicated
- step_alpha: float32 [512], replicated
- res_norm: float32 [512], replicated
Inputs may be any that keep to these rules, and one draw needn't show every extreme that they name: `face_len`: two subdomains that share a face have equal lengths on it; faces on the outer ends of lat and depth have length 0. `residual`: the two copies of a shared interface row are equal, and rows past a face's length are zero. `prev_direction`: the two copies of a shared interface row are equal, and rows past a face's length are zero. `schur`: each matrix has a positive definite symmetric part. `neumann`: each matrix has a positive definite symmetric part. `coarse_inverse`: each matrix has a positive definite symmetric part. `prim_owner`: at most 24 primal dofs of one subdomain have the same owner.
All inputs are finite; a program needn't handle non-finite values.
Results may differ from a plain program's by a relative error of at most 0.00005.
Values sent between devices are 32-bit elements; how exact they have to be, the bound alone decides.
A program may use at most 64 MiB of HBM per device.

v0:
```python
import jax
import jax.numpy as jnp
from jax import lax
from jax.sharding import PartitionSpec as P

CAP = 24


exact_mode = lax.Precision.HIGHEST


def from_behind(x, axis, by):
    devices = lax.axis_size(axis)
    return lax.ppermute(x, axis, [(i, (i + by) % devices) for i in range(devices)])


def passed_along(block, axis, distance):
    devices = range(lax.axis_size(axis))
    route = [(i - distance, i) for i in devices if i - distance in devices]
    return lax.ppermute(block, axis, route)


def product(left, right):
    return jnp.dot(left, right, precision=exact_mode, preferred_element_type=jnp.float32)


def product_t(left, right):
    return lax.dot_general(
        left,
        right,
        (((0,), (0,)), ((), ())),
        precision=exact_mode,
        preferred_element_type=jnp.float32,
    )


def assemble(vector, live_mask):
    col_count = vector.shape[1]
    face_rows = vector.shape[0] // 6
    face_list = vector.reshape(6, face_rows, col_count)
    received = [None] * 6
    for facing in range(2):
        shift_by = 1 - 2 * facing
        received[facing] = from_behind(face_list[1 - facing], "blk", shift_by)
        received[2 + facing] = passed_along(face_list[3 - facing], "lat", shift_by)
        received[4 + facing] = passed_along(face_list[5 - facing], "depth", shift_by)
    return live_mask * (vector + jnp.stack(received).reshape(vector.shape))


def coarse_level(coarse_terms, owner_ids, row_ids, inverse):
    primal, col_count = coarse_terms.shape
    owners = lax.axis_size(("blk", "lat"))
    slots = owners * CAP
    owner_hit = (owner_ids[:, None] == lax.broadcasted_iota(jnp.int32, (primal, owners), 1)).astype(
        jnp.int32
    )
    owner_rank = jnp.sum(jnp.cumsum(owner_hit, axis=0) * owner_hit, axis=1) - 1
    slot_index = owner_ids * CAP + owner_rank
    packer = slot_index[None, :] == lax.broadcasted_iota(jnp.int32, (slots, primal), 0)
    pack_table = packer.astype(jnp.float32)
    outgoing = product(pack_table, coarse_terms).reshape(owners, CAP, col_count)
    outgoing_rows = (jnp.sum(jnp.where(packer, row_ids[None, :] + 1, 0), axis=1) - 1).reshape(
        owners, CAP
    )
    incoming, incoming_rows = (
        lax.all_to_all(outgoing, ("blk", "lat"), split_axis=0, concat_axis=0, tiled=True),
        lax.all_to_all(outgoing_rows, ("blk", "lat"), split_axis=0, concat_axis=0, tiled=True),
    )
    owned_rows = inverse.shape[0]
    picker = (
        incoming_rows.reshape(1, slots) == lax.broadcasted_iota(jnp.int32, (owned_rows, slots), 0)
    ).astype(jnp.float32)
    gathered = product(picker, incoming.reshape(slots, col_count))
    solved = product(inverse, gathered)
    answers = product_t(picker, solved)
    returned = lax.all_to_all(
        answers.reshape(owners, CAP, col_count),
        ("blk", "lat"),
        split_axis=0,
        concat_axis=0,
        tiled=True,
    )
    return product_t(pack_table, returned.reshape(slots, col_count))


def shards(
    face_len,
    residual,
    prev_direction,
    prev_rho,
    schur,
    neumann,
    coarse_basis,
    coarse_inverse,
    prim_owner,
    coarse_row,
):
    row_count = residual.shape[3]
    col_count = residual.shape[4]
    face_rows = row_count // 6
    primal = coarse_basis.shape[4]
    owned_rows = coarse_inverse.shape[3]
    lengths = face_len.reshape(6)
    live_mask = (
        (lax.broadcasted_iota(jnp.int32, (6, face_rows), 1) < lengths[:, None])
        .astype(jnp.float32)
        .reshape(row_count, 1)
    )
    residual_live = live_mask * residual.reshape(row_count, col_count)
    weighted = 0.5 * residual_live
    local_part = product(neumann.reshape(row_count, row_count), weighted)
    basis = coarse_basis.reshape(row_count, primal)
    coarse_terms = product_t(basis, weighted)
    correction = coarse_level(
        coarse_terms,
        prim_owner.reshape(primal),
        coarse_row.reshape(primal),
        coarse_inverse.reshape(owned_rows, owned_rows),
    )
    precond_image = local_part + product(basis, correction)
    precond = 0.5 * assemble(precond_image, live_mask)
    devices = lax.axis_size(("blk", "lat", "depth"))
    norm_scale = 0.5 / (devices * row_count)
    rho_now = norm_scale * lax.psum(
        jnp.sum(residual_live * precond, axis=0), ("blk", "lat", "depth")
    )
    direction = precond + rho_now / prev_rho * (
        live_mask * prev_direction.reshape(row_count, col_count)
    )
    schur_image = product(schur.reshape(row_count, row_count), direction)
    applied = assemble(schur_image, live_mask)
    curv_sum = lax.psum(jnp.sum(direction * applied, axis=0), ("blk", "lat", "depth"))
    step_alpha = rho_now / (norm_scale * curv_sum)
    new_residual = residual_live - step_alpha * applied
    res_norm = norm_scale * lax.psum(
        jnp.sum(new_residual * new_residual, axis=0), ("blk", "lat", "depth")
    )
    out_shape = (1, 1, 1, row_count, col_count)
    return (
        new_residual.reshape(out_shape),
        direction.reshape(out_shape),
        rho_now,
        step_alpha,
        res_norm,
    )


def solution(mesh):
    in_specs = (
        P("blk", "lat", "depth", None),
        P("blk", "lat", "depth", None, None),
        P("blk", "lat", "depth", None, None),
        P(),
        P("blk", "lat", "depth", None, None),
        P("blk", "lat", "depth", None, None),
        P("blk", "lat", "depth", None, None),
        P("blk", "lat", "depth", None, None),
        P("blk", "lat", "depth", None, None),
        P("blk", "lat", "depth", None),
    )
    out_specs = (
        P("blk", "lat", "depth", None, None),
        P("blk", "lat", "depth", None, None),
        P(),
        P(),
        P(),
    )
    return jax.shard_map(shards, mesh=mesh, in_specs=in_specs, out_specs=out_specs, check_vma=False)
```

profile of v0, /device:TPU:1, one launch (start us, length us, event | category | flops | bytes accessed | tf_op | source)
XLA Modules:
  0.0 437.7 jit_solution(7040188213010964891)
XLA Ops:
  5.3 11.9 %all-to-all-start = ((s32[32,1,24]{2,1,0:T(1,128)}), s32[32,1,24]{2,1,0:T(1,128)S(1)}, u32[]{:S(2)}, u32[]{:S(2)}) async-start(s32[32,1,24]{2,1,0:T(1,128)} %bitcast.9), calls=%async_computation | async-start | bytes 32768 | tf_op jit(solution)/shard_map/all_to_all | solution.py:67
  17.9 4.4 %fusion.6 = f32[512,256]{1,0:T(8,128)S(1)} fusion(f32[1,1,1,768,512]{4,3,2,1,0:T(8,128)} %param.11, f32[1,1,1,768,256]{4,3,2,1,0:T(8,128)} %param.16, f32[768]{0:T(1024)S(1)} %convert_bitcast_fusion), kind=kOutput, calls=%fused_computation.7 | convolution fusion | flops 1208745984 | bytes 2886656 | tf_op jit(solution)/shard_map/dot_general | solution.py:28
  25.7 7.9 %all-to-all-start.1 = ((f32[32,24,512]{2,1,0:T(8,128)}), f32[32,24,512]{2,1,0:T(8,128)}, u32[]{:S(2)}, u32[]{:S(2)}) async-start(f32[32,24,512]{2,1,0:T(8,128)} %bitcast.103), calls=%async_computation.1 | async-start | bytes 3145728 | tf_op jit(solution)/shard_map/all_to_all | solution.py:66
  34.9 35.1 %all-to-all-done.1 = f32[32,24,512]{2,1,0:T(8,128)} async-done(((f32[32,24,512]{2,1,0:T(8,128)}), f32[32,24,512]{2,1,0:T(8,128)}, u32[]{:S(2)}, u32[]{:S(2)}) %all-to-all-start.1) | async-done | bytes 1572896 | tf_op jit(solution)/shard_map/all_to_all | solution.py:66
  70.1 2.4 fusion.15
  73.5 2.1 fusion.22
  75.6 7.3 %all-to-all-start.2 = ((f32[32,24,512]{2,1,0:T(8,128)}), f32[32,24,512]{2,1,0:T(8,128)}, u32[]{:S(2)}, u32[]{:S(2)}) async-start(f32[32,24,512]{2,1,0:T(8,128)} %bitcast.100), calls=%async_computation.2 | async-start | bytes 3145728 | tf_op jit(solution)/shard_map/all_to_all | solution.py:76
  82.9 10.3 %fusion.2 = f32[512,768]{1,0:T(8,128)} fusion(f32[1,1,1,768,768]{4,3,2,1,0:T(8,128)S(1)} %copy-done, f32[1,1,1,768,512]{4,3,2,1,0:T(8,128)} %param.11, f32[768]{0:T(1024)S(1)} %convert_bitcast_fusion), kind=kOutput, calls=%fused_computation.2 | convolution fusion | flops 3624665088 | bytes 5508096 | tf_op jit(solution)/shard_map/dot_general | solution.py:24
  93.2 25.3 %all-to-all-done.2 = f32[32,24,512]{2,1,0:T(8,128)} async-done(((f32[32,24,512]{2,1,0:T(8,128)}), f32[32,24,512]{2,1,0:T(8,128)}, u32[]{:S(2)}, u32[]{:S(2)}) %all-to-all-start.2) | async-done | bytes 1572896 | tf_op jit(solution)/shard_map/all_to_all | solution.py:76
  118.5 2.5 fusion.16
  121.1 2.6 add_bitcast_fusion
  127.7 3.0 copy.40
  130.7 3.0 copy.45
  133.8 5.3 %collective-permute-start.2 = (f32[128,512]{0,1:T(8,128)S(1)}, f32[128,512]{0,1:T(8,128)S(1)}, u32[]{:S(2)}, u32[]{:S(2)}) collective-permute-start(f32[128,512]{0,1:T(8,128)S(1)} %get-tuple-element.38), channel_id=1, source_target_pairs={{0,8},{8,16},{16,24},{1,9},{9,17},{17,25},{2,10},{10,18},{18,26},{... | collective-permute-start | bytes 786440 | tf_op jit(solution)/shard_map/ppermute | solution.py:20
  140.4 5.9 %collective-permute-start.4 = (f32[128,512]{0,1:T(8,128)S(1)}, f32[128,512]{0,1:T(8,128)S(1)}, u32[]{:S(2)}, u32[]{:S(2)}) collective-permute-start(f32[128,512]{0,1:T(8,128)S(1)} %get-tuple-element.36), channel_id=1, source_target_pairs={{0,1},{1,2},{2,3},{3,4},{4,5},{5,6},{6,7},{8,9},{9,10},{10,11},{11... | collective-permute-start | bytes 786440 | tf_op jit(solution)/shard_map/ppermute | solution.py:20
  154.8 3.0 copy.43
  157.8 3.0 copy.44
  160.8 2.7 multiply_reduce_fusion.2
  163.6 75.6 %psum.21 = f32[512]{0:T(512)S(1)} all-reduce(f32[512]{0:T(512)S(1)} %multiply_reduce_fusion.2), channel_id=1, replica_groups=mesh['blk'=8,'lat'=4,'depth'=8] {'blk','lat','depth'}, use_global_device_ids=true, to_apply=%region_5.6 | all-reduce | flops 512 | bytes 4096 | tf_op jit(solution)/shard_map/psum | solution.py:124
  239.2 2.9 fusion.5
  242.3 4.0 fusion.9
  250.4 2.9 collective-permute-start.8
  254.6 2.6 collective-permute-start.10
  257.2 3.0 copy.49
  260.2 3.0 collective-permute-start.11
  272.4 3.1 copy.46
  275.4 3.0 copy.47
  278.5 2.6 multiply_reduce_fusion.1
  281.1 74.9 %psum.22 = f32[512]{0:T(512)S(1)} all-reduce(f32[512]{0:T(512)S(1)} %multiply_reduce_fusion.1), channel_id=1, replica_groups=mesh['blk'=8,'lat'=4,'depth'=8] {'blk','lat','depth'}, use_global_device_ids=true, to_apply=%region_7.8 | all-reduce | flops 512 | bytes 4096 | tf_op jit(solution)/shard_map/psum | solution.py:132
  356.0 3.9 multiply_reduce_fusion
  359.9 3.0 copy.48
  362.9 74.2 %psum.23 = f32[512]{0:T(512)S(1)} all-reduce(f32[512]{0:T(512)S(1)} %get-tuple-element.25), channel_id=1, replica_groups=mesh['blk'=8,'lat'=4,'depth'=8] {'blk','lat','depth'}, use_global_device_ids=true, to_apply=%region_9.10 | all-reduce | flops 512 | bytes 4096 | tf_op jit(solution)/shard_map/psum | solution.py:135
  (76 shorter events, 40.0 us)
Async XLA Ops:
  0.6 82.2 %copy-start = (f32[1,1,1,768,768]{4,3,2,1,0:T(8,128)S(1)}, f32[1,1,1,768,768]{4,3,2,1,0:T(8,128)}, u32[]{:S(2)}) copy-start(f32[1,1,1,768,768]{4,3,2,1,0:T(8,128)} %param.15) | copy-start | bytes 7077892
  5.3 20.4 %all-to-all-start = ((s32[32,1,24]{2,1,0:T(1,128)}), s32[32,1,24]{2,1,0:T(1,128)S(1)}, u32[]{:S(2)}, u32[]{:S(2)}) async-start(s32[32,1,24]{2,1,0:T(1,128)} %bitcast.9), calls=%async_computation | async-start | bytes 32768 | tf_op jit(solution)/shard_map/all_to_all | solution.py:67
  25.7 44.4 %all-to-all-start.1 = ((f32[32,24,512]{2,1,0:T(8,128)}), f32[32,24,512]{2,1,0:T(8,128)}, u32[]{:S(2)}, u32[]{:S(2)}) async-start(f32[32,24,512]{2,1,0:T(8,128)} %bitcast.103), calls=%async_computation.1 | async-start | bytes 3145728 | tf_op jit(solution)/shard_map/all_to_all | solution.py:66
  33.6 38.8 %copy-start.7 = (f32[1,1,1,256,256]{4,3,2,1,0:T(8,128)S(1)}, f32[1,1,1,256,256]{4,3,2,1,0:T(8,128)}, u32[]{:S(2)}) copy-start(f32[1,1,1,256,256]{4,3,2,1,0:T(8,128)} %param.17) | copy-start | bytes 786436
  75.6 42.9 %all-to-all-start.2 = ((f32[32,24,512]{2,1,0:T(8,128)}), f32[32,24,512]{2,1,0:T(8,128)}, u32[]{:S(2)}, u32[]{:S(2)}) async-start(f32[32,24,512]{2,1,0:T(8,128)} %bitcast.100), calls=%async_computation.2 | async-start | bytes 3145728 | tf_op jit(solution)/shard_map/all_to_all | solution.py:76
  82.9 38.2 %copy-start.5 = (f32[1,1,1,768,256]{4,3,2,1,0:T(8,128)S(1)}, f32[1,1,1,768,256]{4,3,2,1,0:T(8,128)}, u32[]{:S(2)}) copy-start(f32[1,1,1,768,256]{4,3,2,1,0:T(8,128)} %param.16) | copy-start | bytes 2359300
  118.5 2.6 copy-start.4
  123.7 1.3 copy-start.2
  125.0 21.3 %collective-permute-start = (f32[128,512]{0,1:T(8,128)}, f32[128,512]{0,1:T(8,128)}, u32[]{:S(2)}, u32[]{:S(2)}) collective-permute-start(f32[128,512]{0,1:T(8,128)} %get-tuple-element.40), channel_id=1, source_target_pairs={{0,32},{32,64},{64,96},{96,128},{128,160},{160,192},{192,224},{224... | collective-permute-start | bytes 786440 | tf_op jit(solution)/shard_map/ppermute | solution.py:14
  125.8 24.2 %collective-permute-start.1 = (f32[128,512]{0,1:T(8,128)}, f32[128,512]{0,1:T(8,128)}, u32[]{:S(2)}, u32[]{:S(2)}) collective-permute-start(f32[128,512]{0,1:T(8,128)} %get-tuple-element.39), channel_id=1, source_target_pairs={{0,224},{32,0},{64,32},{96,64},{128,96},{160,128},{192,160},{224,1... | collective-permute-start | bytes 786440 | tf_op jit(solution)/shard_map/ppermute | solution.py:14
  133.8 17.9 %collective-permute-start.2 = (f32[128,512]{0,1:T(8,128)S(1)}, f32[128,512]{0,1:T(8,128)S(1)}, u32[]{:S(2)}, u32[]{:S(2)}) collective-permute-start(f32[128,512]{0,1:T(8,128)S(1)} %get-tuple-element.38), channel_id=1, source_target_pairs={{0,8},{8,16},{16,24},{1,9},{9,17},{17,25},{2,10},{10,18},{18,26},{... | collective-permute-start | bytes 786440 | tf_op jit(solution)/shard_map/ppermute | solution.py:20
  139.1 13.3 %collective-permute-start.3 = (f32[128,512]{0,1:T(8,128)S(1)}, f32[128,512]{0,1:T(8,128)S(1)}, u32[]{:S(2)}, u32[]{:S(2)}) collective-permute-start(f32[128,512]{0,1:T(8,128)S(1)} %get-tuple-element.37), channel_id=1, source_target_pairs={{8,0},{16,8},{24,16},{9,1},{17,9},{25,17},{10,2},{18,10},{26,18},{... | collective-permute-start | bytes 786440 | tf_op jit(solution)/shard_map/ppermute | solution.py:20
  140.4 12.7 %collective-permute-start.4 = (f32[128,512]{0,1:T(8,128)S(1)}, f32[128,512]{0,1:T(8,128)S(1)}, u32[]{:S(2)}, u32[]{:S(2)}) collective-permute-start(f32[128,512]{0,1:T(8,128)S(1)} %get-tuple-element.36), channel_id=1, source_target_pairs={{0,1},{1,2},{2,3},{3,4},{4,5},{5,6},{6,7},{8,9},{9,10},{10,11},{11... | collective-permute-start | bytes 786440 | tf_op jit(solution)/shard_map/ppermute | solution.py:20
  146.4 7.7 %collective-permute-start.5 = (f32[128,512]{0,1:T(8,128)S(1)}, f32[128,512]{0,1:T(8,128)S(1)}, u32[]{:S(2)}, u32[]{:S(2)}) collective-permute-start(f32[128,512]{0,1:T(8,128)S(1)} %get-tuple-element.35), channel_id=1, source_target_pairs={{1,0},{2,1},{3,2},{4,3},{5,4},{6,5},{7,6},{9,8},{10,9},{11,10},{12... | collective-permute-start | bytes 786440 | tf_op jit(solution)/shard_map/ppermute | solution.py:20
  160.8 78.4 %copy-start.10 = (f32[512]{0:T(512)S(1)}, f32[512]{0:T(512)}, u32[]{:S(2)}) copy-start(f32[512]{0:T(512)} %param.13) | copy-start | bytes 6148
  239.2 116.8 %copy-start.9 = (f32[512]{0:T(512)}, f32[512]{0:T(512)S(1)}, u32[]{:S(2)}) copy-start(f32[512]{0:T(512)S(1)} %get-tuple-element.28) | copy-start | bytes 6148
  239.2 3.1 copy-start.6
  242.3 4.1 copy-start.3
  246.4 1.3 copy-start.1
  247.7 12.6 %collective-permute-start.6 = (f32[128,512]{0,1:T(8,128)}, f32[128,512]{0,1:T(8,128)}, u32[]{:S(2)}, u32[]{:S(2)}) collective-permute-start(f32[128,512]{0,1:T(8,128)} %get-tuple-element.34), channel_id=1, source_target_pairs={{0,32},{32,64},{64,96},{96,128},{128,160},{160,192},{192,224},{224... | collective-permute-start | bytes 786440 | tf_op jit(solution)/shard_map/ppermute | solution.py:14
  249.5 15.5 %collective-permute-start.7 = (f32[128,512]{0,1:T(8,128)}, f32[128,512]{0,1:T(8,128)}, u32[]{:S(2)}, u32[]{:S(2)}) collective-permute-start(f32[128,512]{0,1:T(8,128)} %get-tuple-element.33), channel_id=1, source_target_pairs={{0,224},{32,0},{64,32},{96,64},{128,96},{160,128},{192,160},{224,1... | collective-permute-start | bytes 786440 | tf_op jit(solution)/shard_map/ppermute | solution.py:14
  250.4 16.3 %collective-permute-start.8 = (f32[128,512]{0,1:T(8,128)S(1)}, f32[128,512]{0,1:T(8,128)}, u32[]{:S(2)}, u32[]{:S(2)}) collective-permute-start(f32[128,512]{0,1:T(8,128)S(1)} %get-tuple-element.32), channel_id=1, source_target_pairs={{0,8},{8,16},{16,24},{1,9},{9,17},{17,25},{2,10},{10,18},{18,26},{... | collective-permute-start | bytes 786440 | tf_op jit(solution)/shard_map/ppermute | solution.py:20
  253.3 15.0 %collective-permute-start.9 = (f32[128,512]{0,1:T(8,128)S(1)}, f32[128,512]{0,1:T(8,128)}, u32[]{:S(2)}, u32[]{:S(2)}) collective-permute-start(f32[128,512]{0,1:T(8,128)S(1)} %get-tuple-element.31), channel_id=1, source_target_pairs={{8,0},{16,8},{24,16},{9,1},{17,9},{25,17},{10,2},{18,10},{26,18},{... | collective-permute-start | bytes 786440 | tf_op jit(solution)/shard_map/ppermute | solution.py:20
  254.6 15.4 %collective-permute-start.10 = (f32[128,512]{0,1:T(8,128)S(1)}, f32[128,512]{0,1:T(8,128)}, u32[]{:S(2)}, u32[]{:S(2)}) collective-permute-start(f32[128,512]{0,1:T(8,128)S(1)} %get-tuple-element.30), channel_id=1, source_target_pairs={{0,1},{1,2},{2,3},{3,4},{4,5},{5,6},{6,7},{8,9},{9,10},{10,11},{11... | collective-permute-start | bytes 786440 | tf_op jit(solution)/shard_map/ppermute | solution.py:20
  260.2 11.4 %collective-permute-start.11 = (f32[128,512]{0,1:T(8,128)S(1)}, f32[128,512]{0,1:T(8,128)S(1)}, u32[]{:S(2)}, u32[]{:S(2)}) collective-permute-start(f32[128,512]{0,1:T(8,128)S(1)} %get-tuple-element.29), channel_id=1, source_target_pairs={{1,0},{2,1},{3,2},{4,3},{5,4},{6,5},{7,6},{9,8},{10,9},{11,10},{12... | collective-permute-start | bytes 786440 | tf_op jit(solution)/shard_map/ppermute | solution.py:20
  356.0 3.9 copy-start.8
where the time goes:
time: 439 us; the launch traced here: 438 us
  blocking collectives  225 us (51%)
  waiting for transfers between devices  62.1 us (14%)
  starting transfers between devices  56.7 us (13%)
  local copies, waits for them, and re-layouts  43.9 us (10%)
  matrix products  31.4 us (7%)
  other arithmetic  18 us (4%)
    psum x1, blocking collectives, shards(): lax.psum(jnp.sum(residual_live * precond, axis=0), ('blk', 'lat', 'depth'))  75.6 us
    psum x1, blocking collectives, shards(): lax.psum(jnp.sum(direction * applied, axis=0), ('blk', 'lat', 'depth'))  74.9 us
    psum x1, blocking collectives, shards(): lax.psum(jnp.sum(new_residual * new_residual, axis=0), ('blk', 'lat', 'de...  74.2 us
    all_to_all x1, waiting for transfers between devices, coarse_level(): lax.all_to_all(outgoing, ('blk', 'lat'), split_axis=0, concat_axis=0, til...  35.1 us
    unnamed x36, local copies, waits for them, and re-layouts  26.8 us
    all_to_all x1, waiting for transfers between devices, coarse_level(): lax.all_to_all(answers.reshape(owners, CAP, col_count), ('blk', 'lat'), s...  25.3 us
    ppermute x8, starting transfers between devices, passed_along(): return lax.ppermute(block, axis, route)  24.4 us
    dot_general x6, matrix products, product(): jnp.dot(left, right, precision=exact_mode, preferred_element_type=jnp.flo...  22.3 us
  transfers between devices with their start and end apart: 15, of which 4 were waited for; matrix products, arithmetic and copies ran while one was open for 10% of the time, Pallas kernels for 0%

commit v1 on v0

v1 whole, which is shorter than its diff:
```python
import functools
import jax
import jax.numpy as jnp
from jax import lax
from jax.experimental import pallas as pl
from jax.experimental.pallas import tpu as pltpu
from jax.sharding import PartitionSpec as P

CAP = 24
STRIDE = 32
F32 = jnp.float32
BF16 = jnp.bfloat16
MESH = pl.DeviceIdType.MESH


def split(x):
    hi = x.astype(BF16)
    return hi, (x - hi.astype(F32)).astype(BF16)


def mm(a, b):
    return lax.dot_general(a, b, (((1,), (0,)), ((), ())), preferred_element_type=F32)


def mm3(a, bh, bl):
    ah, al = split(a)
    return mm(ah, bh) + (mm(ah, bl) + mm(al, bh))


def iota(shape, dim):
    return lax.broadcasted_iota(jnp.int32, shape, dim)


def step_kernel(
    sizes,
    norm_scale,
    fl_ref,
    own_ref,
    crow_ref,
    prho_ref,
    r_hbm,
    pp_hbm,
    s_hbm,
    n_hbm,
    phi_hbm,
    c_hbm,
    nr_hbm,
    dir_hbm,
    rho_ref,
    alpha_ref,
    norm_ref,
    r_v,
    pp_v,
    s_v,
    n_v,
    phi_v,
    c_v,
    wh_v,
    wl_v,
    th_v,
    tl_v,
    slotr_v,
    slotc_v,
    pick_v,
    pickt_v,
    rows_out,
    rows_in,
    out_buf,
    in_buf,
    rel1,
    ans_buf,
    ret_buf,
    rel2,
    gath_v,
    nloc_v,
    img_v,
    rx1,
    p_v,
    simg_v,
    rx2,
    ar_src,
    ar_a,
    ar_b,
    ar_mid,
    ld_sem,
    row_s,
    row_r,
    x_s,
    x_r,
    rel_s,
    rel_r,
    fwd_s,
    ara_s,
    ara_r,
    arb_s,
    arb_r,
    f_s,
    f_r,
    own_sem,
    o_sem,
):
    n_blk, n_lat, n_depth = sizes
    owners = n_blk * n_lat
    b, l, d = lax.axis_index("blk"), lax.axis_index("lat"), lax.axis_index("depth")
    me = b * n_lat + l
    nb, nr = r_v.shape
    face = nb // 6
    nc = phi_v.shape[1]
    co = c_v.shape[0]
    half = n_blk // 2
    quarter = n_blk // 4

    def load(src, dst, k):
        return pltpu.make_async_copy(src, dst, ld_sem.at[k])

    loads = [
        load(r_hbm, r_v, 0),
        load(phi_hbm, phi_v, 1),
        load(n_hbm, n_v, 2),
        load(c_hbm, c_v, 3),
        load(pp_hbm, pp_v, 4),
        load(s_hbm, s_v, 5),
    ]
    for one in loads:
        one.start()

    in_buf[:, CAP:, :] = jnp.zeros((owners, STRIDE - CAP, nr), F32)

    def peer(k):
        db, j = k // n_lat, k % n_lat
        return lax.rem(b + db, n_blk), lax.rem(l + j, n_lat)

    barrier = pltpu.get_barrier_semaphore()

    def greet(k, c):
        pb, plat = peer(k)
        pl.semaphore_signal(barrier, inc=1, device_id=(pb, plat, d), device_id_type=MESH)
        return c

    lax.fori_loop(1, owners, greet, 0)

    def greet_depth(k, c):
        pl.semaphore_signal(
            barrier, inc=1, device_id=(b, l, lax.rem(d + k, n_depth)), device_id_type=MESH
        )
        return c

    lax.fori_loop(1, n_depth, greet_depth, 0)

    own_row = own_ref[...]
    own_b = jnp.broadcast_to(own_row.astype(F32), (nc, nc))
    own_t = jnp.transpose(own_b)
    ii, jj = iota((nc, nc), 0), iota((nc, nc), 1)
    same = own_b == own_t
    rank_row = jnp.sum(jnp.where(same & (ii < jj), 1.0, 0.0), axis=0, keepdims=True)
    rank_col = jnp.sum(jnp.where(same & (jj < ii), 1.0, 0.0), axis=1, keepdims=True)
    slotr_v[...] = own_row * CAP + rank_row.astype(jnp.int32)
    slotc_v[...] = (own_t * CAP + rank_col).astype(jnp.int32)
    left = jnp.where(
        jnp.broadcast_to(own_row, (owners, nc)) == iota((owners, nc), 0),
        jnp.broadcast_to((crow_ref[...] + 1).astype(F32), (owners, nc)),
        0.0,
    ).astype(BF16)
    right = jnp.where(
        rank_col.astype(jnp.int32) + STRIDE * l == iota((nc, 4 * STRIDE), 1), 1.0, 0.0
    ).astype(BF16)
    table = mm(left, right)
    for o in range(owners):
        rows_out[o] = table[o : o + 1, :]

    loads[0].wait()
    for f in range(6):
        rows = pl.ds(f * face, face)
        live = iota((face, nr), 0) < fl_ref[f]
        rl = jnp.where(live, r_v[rows, :], 0.0)
        r_v[rows, :] = rl
        wh, wl = split(0.5 * rl)
        wh_v[rows, :] = wh
        wl_v[rows, :] = wl
    loads[1].wait()
    terms = mm3(jnp.transpose(phi_v[...]), wh_v[...], wl_v[...])
    th, tl = split(terms)
    th_v[...] = th
    tl_v[...] = tl

    pl.semaphore_wait(barrier, owners - 1 + n_depth - 1)

    def rows_copy(k, c):
        pb, plat = peer(k)
        pltpu.make_async_remote_copy(
            src_ref=rows_out.at[pb * n_lat + plat],
            dst_ref=rows_in.at[me],
            send_sem=row_s.at[0],
            recv_sem=row_r.at[0],
            device_id=(pb, plat, d),
            device_id_type=MESH,
        ).start()
        return c

    lax.fori_loop(1, owners, rows_copy, 0)
    pltpu.make_async_copy(rows_out.at[me], rows_in.at[me], row_r.at[0]).start()

    def tile_copy(src, dst, way, dev):
        return pltpu.make_async_remote_copy(
            src_ref=src,
            dst_ref=dst,
            send_sem=x_s.at[way],
            recv_sem=x_r.at[way],
            device_id=dev,
            device_id_type=MESH,
        )

    def tile_sends(src_of, dst_of, rel, way, db):
        tb = lax.rem(b + db, n_blk)
        for j in range(n_lat):
            tl_ = lax.rem(l + j, n_lat)
            src = src_of(tb * n_lat + tl_)
            if db == half:
                via = quarter if j < n_lat // 2 else n_blk - quarter
                pltpu.make_async_remote_copy(
                    src_ref=src,
                    dst_ref=rel.at[j],
                    send_sem=rel_s.at[way],
                    recv_sem=rel_r.at[way],
                    device_id=(lax.rem(b + via, n_blk), l, d),
                    device_id_type=MESH,
                ).start()
            elif db == 0 and j == 0:
                pltpu.make_async_copy(src, dst_of(me), x_r.at[way]).start()
            else:
                tile_copy(src, dst_of(me), way, (tb, tl_, d)).start()

    def tile_forward(dst_of, rel, way):
        pltpu.make_async_copy(rel, rel, rel_r.at[way]).wait()
        for j in range(n_lat):
            go = quarter if j < n_lat // 2 else n_blk - quarter
            origin = lax.rem(b + n_blk - go, n_blk) * n_lat + l
            pltpu.make_async_remote_copy(
                src_ref=rel.at[j],
                dst_ref=dst_of(origin),
                send_sem=fwd_s.at[way],
                recv_sem=x_r.at[way],
                device_id=(lax.rem(b + go, n_blk), lax.rem(l + j, n_lat), d),
                device_id_type=MESH,
            ).start()

    order = [half]
    for step in range(half - 1, 0, -1):
        order += [step, n_blk - step]
    order += [0]

    out_of = lambda o: out_buf.at[o]
    in_of = lambda o: in_buf.at[o, pl.ds(0, CAP)]
    ans_of = lambda o: ans_buf.at[o, pl.ds(0, CAP)]
    ret_of = lambda o: ret_buf.at[o]

    chunk = n_lat * CAP
    for db in order:
        tb = lax.rem(b + db, n_blk)
        pack = jnp.where(
            iota((chunk, nc), 0) + tb * chunk == jnp.broadcast_to(slotr_v[...], (chunk, nc)),
            1.0,
            0.0,
        ).astype(BF16)
        tiles = mm(pack, th_v[...]) + mm(pack, tl_v[...])
        out_buf[pl.ds(tb * n_lat, n_lat)] = tiles.reshape(n_lat, CAP, nr)
        tile_sends(out_of, in_of, rel1, 0, db)

    loads[2].wait()

    def local_block(f, acc):
        rows = pl.ds(pl.multiple_of(f * face, face), face)
        y = mm3(n_v[rows, :], wh_v[...], wl_v[...])
        nloc_v[rows, :] = y
        return acc + jnp.sum(r_v[rows, :] * y, axis=0, keepdims=True)

    rho_local = lax.fori_loop(0, 3, local_block, jnp.zeros((1, nr), F32))
    tile_forward(in_of, rel1, 0)
    rho_local = lax.fori_loop(3, 6, local_block, rho_local)
    ar_src[0] = rho_local

    pltpu.make_async_copy(rows_in, rows_in, row_r.at[0]).wait()
    wide = n_lat * STRIDE
    for g in range(n_blk):
        v = rows_in[g * n_lat]
        for j in range(1, n_lat):
            v = v + rows_in[g * n_lat + j]
        v = v - 1.0
        pick_v[:, pl.ds(g * wide, wide)] = jnp.where(
            jnp.broadcast_to(v, (co, wide)) == iota((co, wide), 0).astype(F32), 1.0, 0.0
        ).astype(BF16)
        vt = jnp.transpose(jnp.broadcast_to(v, (wide, wide)))
        for c in range(co // wide):
            pickt_v[g, :, pl.ds(c * wide, wide)] = jnp.where(
                vt == (iota((wide, wide), 1) + c * wide).astype(F32), 1.0, 0.0
            ).astype(BF16)
    loads[3].wait()

    pltpu.make_async_copy(in_of(slice(None)), in_of(slice(None)), x_r.at[0]).wait()
    per = 2 * n_lat
    for g in range(n_blk // 2):
        xh, xl = split(in_buf[pl.ds(g * per, per)].reshape(per * STRIDE, nr))
        pick = pick_v[:, pl.ds(g * 2 * wide, 2 * wide)]
        part = mm(pick, xh) + mm(pick, xl)
        if g == 0:
            gath_v[...] = part
        else:
            gath_v[...] += part
    gathered = gath_v[...]
    gh, gl = split(gathered)
    solved = mm3(c_v[...], gh, gl)
    ar_src[0] += 2.0 * jnp.sum(gathered * solved, axis=0, keepdims=True)
    sh, sl = split(solved)
    th_v[...] = sh
    tl_v[...] = sl

    def reduce_start(k):
        def send(i, c):
            pb, plat = peer(i)
            pltpu.make_async_remote_copy(
                src_ref=ar_src.at[k],
                dst_ref=ar_a.at[k, me],
                send_sem=ara_s.at[k],
                recv_sem=ara_r.at[k],
                device_id=(pb, plat, d),
                device_id_type=MESH,
            ).start()
            return c

        lax.fori_loop(1, owners, send, 0)
        pltpu.make_async_copy(ar_src.at[k], ar_a.at[k, me], ara_r.at[k]).start()

    def reduce_middle(k):
        pltpu.make_async_copy(ar_a.at[k], ar_a.at[k], ara_r.at[k]).wait()
        ar_mid[k] = jnp.sum(ar_a[k], axis=0)

        def send(i, c):
            pltpu.make_async_remote_copy(
                src_ref=ar_mid.at[k],
                dst_ref=ar_b.at[k, d],
                send_sem=arb_s.at[k],
                recv_sem=arb_r.at[k],
                device_id=(b, l, lax.rem(d + i, n_depth)),
                device_id_type=MESH,
            ).start()
            return c

        lax.fori_loop(1, n_depth, send, 0)
        pltpu.make_async_copy(ar_mid.at[k], ar_b.at[k, d], arb_r.at[k]).start()

    def reduce_end(k):
        pltpu.make_async_copy(ar_b.at[k], ar_b.at[k], arb_r.at[k]).wait()
        return jnp.sum(ar_b[k], axis=0)

    reduce_start(0)
    for db in order:
        tb = lax.rem(b + db, n_blk)
        pick = pickt_v[tb]
        tiles = mm(pick, th_v[...]) + mm(pick, tl_v[...])
        ans_buf[pl.ds(tb * n_lat, n_lat)] = tiles.reshape(n_lat, STRIDE, nr)
        tile_sends(ans_of, ret_of, rel2, 1, db)
    tile_forward(ret_of, rel2, 1)
    reduce_middle(0)
    rho_now = norm_scale * reduce_end(0)
    rho_ref[...] = rho_now
    beta = rho_now / prho_ref[...]
    loads[4].wait()
    loads[5].wait()

    pltpu.make_async_copy(ret_buf, ret_buf, x_r.at[1]).wait()
    lanes = 8 * CAP
    for g in range(owners // 8):
        yh, yl = split(ret_buf[pl.ds(g * 8, 8)].reshape(lanes, nr))
        pack_t = jnp.where(slotc_v[:, :lanes] == iota((nc, lanes), 1) + g * lanes, 1.0, 0.0).astype(BF16)
        part = mm(pack_t, yh) + mm(pack_t, yl)
        if g == 0:
            gath_v[...] = part
        else:
            gath_v[...] += part
    ch, cl = split(gath_v[...])
    th_v[...] = ch
    tl_v[...] = cl

    def face_send(src, rx, turn, f):
        step = 1 if f % 2 == 1 else -1
        axis = f // 2
        dev = [b, l, d]
        n = sizes[axis]
        dev[axis] = lax.rem(dev[axis] + n + step, n)
        return pltpu.make_async_remote_copy(
            src_ref=src.at[pl.ds(f * face, face)],
            dst_ref=rx.at[f ^ 1],
            send_sem=f_s.at[turn, f],
            recv_sem=f_r.at[turn, f ^ 1],
            device_id=tuple(dev),
            device_id_type=MESH,
        )

    for f in range(6):
        rows = pl.ds(f * face, face)
        img_v[rows, :] = nloc_v[rows, :] + mm3(phi_v[rows, :], th_v[...], tl_v[...])
        face_send(img_v, rx1, 0, f).start()

    for f in (4, 5, 2, 3, 0, 1):
        rows = pl.ds(f * face, face)
        face_send(img_v, rx1, 0, f ^ 1).wait_recv()
        live = iota((face, nr), 0) < fl_ref[f]
        p = jnp.where(live, 0.5 * (img_v[rows, :] + rx1[f]) + beta * pp_v[rows, :], 0.0)
        p_v[rows, :] = p
        ph, plo = split(p)
        wh_v[rows, :] = ph
        wl_v[rows, :] = plo
    dir_out = pltpu.make_async_copy(p_v, dir_hbm, o_sem.at[0])
    dir_out.start()

    def schur_block(f, acc):
        rows = pl.ds(pl.multiple_of(f * face, face), face)
        y = mm3(s_v[rows, :], wh_v[...], wl_v[...])
        simg_v[rows, :] = y
        return acc + jnp.sum(p_v[rows, :] * y, axis=0, keepdims=True)

    ar_src[1] = lax.fori_loop(0, 6, schur_block, jnp.zeros((1, nr), F32))
    reduce_start(1)
    for f in range(6):
        face_send(simg_v, rx2, 1, f).start()
    reduce_middle(1)
    alpha = rho_now / (norm_scale * (2.0 * reduce_end(1)))
    alpha_ref[...] = alpha

    total = jnp.zeros((1, nr), F32)
    for f in (4, 5, 2, 3, 0, 1):
        rows = pl.ds(f * face, face)
        face_send(simg_v, rx2, 1, f ^ 1).wait_recv()
        live = iota((face, nr), 0) < fl_ref[f]
        q = r_v[rows, :] - alpha * jnp.where(live, simg_v[rows, :] + rx2[f], 0.0)
        nloc_v[rows, :] = q
        total = total + jnp.sum(q * q, axis=0, keepdims=True)
    ar_src[2] = total
    reduce_start(2)
    nr_out = pltpu.make_async_copy(nloc_v, nr_hbm, o_sem.at[1])
    nr_out.start()
    reduce_middle(2)
    norm_ref[...] = norm_scale * reduce_end(2)

    dir_out.wait()
    nr_out.wait()
    most = pl.ds(0, owners - 1)

    def left(src, sem):
        pltpu.make_async_copy(src, src, sem).wait()

    left(rows_out.at[most], row_s.at[0])
    direct = pl.ds(0, owners - 1 - n_lat)
    left(out_buf.at[direct], x_s.at[0])
    left(out_buf.at[direct], x_s.at[1])
    for way, rel in ((0, rel1), (1, rel2)):
        left(rel, rel_s.at[way])
        left(rel, fwd_s.at[way])
    for k in range(3):
        left(ar_a.at[k, most], ara_s.at[k])
        left(ar_b.at[k, pl.ds(0, n_depth - 1)], arb_s.at[k])
    for turn, src, rx in ((0, img_v, rx1), (1, simg_v, rx2)):
        for f in range(6):
            face_send(src, rx, turn, f).wait_send()


def shards(
    face_len,
    residual,
    prev_direction,
    prev_rho,
    schur,
    neumann,
    coarse_basis,
    coarse_inverse,
    prim_owner,
    coarse_row,
):
    nb, nr = residual.shape[3:]
    face = nb // 6
    nc = coarse_basis.shape[4]
    co = coarse_inverse.shape[3]
    sizes = tuple(lax.axis_size(a) for a in ("blk", "lat", "depth"))
    owners = sizes[0] * sizes[1]
    devices = owners * sizes[2]
    norm_scale = 0.5 / (devices * nb)
    vm, sem = pltpu.VMEM, pltpu.SemaphoreType.DMA
    whole = pl.BlockSpec(memory_space=pltpu.VMEM)
    far = pl.BlockSpec(memory_space=pl.ANY)
    big = jax.ShapeDtypeStruct((nb, nr), F32)
    small = jax.ShapeDtypeStruct((1, nr), F32)
    scratch = [
        vm((nb, nr), F32),
        vm((nb, nr), F32),
        vm((nb, nb), F32),
        vm((nb, nb), F32),
        vm((nb, nc), F32),
        vm((co, co), F32),
        vm((nb, nr), BF16),
        vm((nb, nr), BF16),
        vm((nc, nr), BF16),
        vm((nc, nr), BF16),
        vm((1, nc), jnp.int32),
        vm((nc, nc), jnp.int32),
        vm((co, owners * STRIDE), BF16),
        vm((sizes[0], sizes[1] * STRIDE, co), BF16),
        vm((owners, 1, 4 * STRIDE), F32),
        vm((owners, 1, 4 * STRIDE), F32),
        vm((owners, CAP, nr), F32),
        vm((owners, STRIDE, nr), F32),
        vm((sizes[1], CAP, nr), F32),
        vm((owners, STRIDE, nr), F32),
        vm((owners, CAP, nr), F32),
        vm((sizes[1], CAP, nr), F32),
        vm((nc, nr), F32),
        vm((nb, nr), F32),
        vm((nb, nr), F32),
        vm((6, face, nr), F32),
        vm((nb, nr), F32),
        vm((nb, nr), F32),
        vm((6, face, nr), F32),
        vm((3, 1, nr), F32),
        vm((3, owners, 1, nr), F32),
        vm((3, sizes[2], 1, nr), F32),
        vm((3, 1, nr), F32),
        sem((6,)),
        sem((1,)),
        sem((1,)),
        sem((2,)),
        sem((2,)),
        sem((2,)),
        sem((2,)),
        sem((2,)),
        sem((3,)),
        sem((3,)),
        sem((3,)),
        sem((3,)),
        sem((2, 6)),
        sem((2, 6)),
        sem((1,)),
        sem((2,)),
    ]
    new_residual, direction, rho_now, step_alpha, res_norm = pl.pallas_call(
        functools.partial(step_kernel, sizes, norm_scale),
        out_shape=(big, big, small, small, small),
        in_specs=[pl.BlockSpec(memory_space=pltpu.SMEM), whole, whole, whole] + [far] * 6,
        out_specs=(far, far, whole, whole, whole),
        scratch_shapes=scratch,
        compiler_params=pltpu.CompilerParams(
            collective_id=0, has_side_effects=True, vmem_limit_bytes=60 * 1024 * 1024
        ),
    )(
        face_len.reshape(6),
        prim_owner.reshape(1, nc),
        coarse_row.reshape(1, nc),
        prev_rho.reshape(1, nr),
        residual.reshape(nb, nr),
        prev_direction.reshape(nb, nr),
        schur.reshape(nb, nb),
        neumann.reshape(nb, nb),
        coarse_basis.reshape(nb, nc),
        coarse_inverse.reshape(co, co),
    )
    out_shape = (1, 1, 1, nb, nr)
    return (
        new_residual.reshape(out_shape),
        direction.reshape(out_shape),
        rho_now.reshape(nr),
        step_alpha.reshape(nr),
        res_norm.reshape(nr),
    )


def solution(mesh):
    deep = P("blk", "lat", "depth", None, None)
    in_specs = (
        P("blk", "lat", "depth", None),
        deep,
        deep,
        P(),
        deep,
        deep,
        deep,
        deep,
        deep,
        P("blk", "lat", "depth", None),
    )
    out_specs = (deep, deep, P(), P(), P())
    return jax.shard_map(shards, mesh=mesh, in_specs=in_specs, out_specs=out_specs, check_vma=False)
```

time: 439 us -> 131 us (0.30)
  blocking collectives: 225 us -> 0 us
  Pallas kernels: 0 us -> 125 us
  waiting for transfers between devices: 62.1 us -> 0 us
  starting transfers between devices: 56.7 us -> 0 us
  local copies, waits for them, and re-layouts: 43.9 us -> 5.68 us
  matrix products: 31.4 us -> 0 us
  other arithmetic: 18 us -> 0 us
    psum x3 -> x0, blocking collectives: 225 us -> none  [the longest x1 75.6 us: shards(): lax.psum(jnp.sum(residual_live * precond, axis=0), ('blk', 'lat', 'depth'))]
    pallas_call x0 -> x1, Pallas kernels: none -> 125 us  [shards(): pl.pallas_call(functools.partial(step_kernel, sizes, norm_scale), out_sha...]
    all_to_all x3 -> x0, waiting for transfers between devices: 61.9 us -> none  [the longest x1 35.1 us: coarse_level(): lax.all_to_all(outgoing, ('blk', 'lat'), split_axis=0, concat_axis=0, til...]
    dot_general x9 -> x0, matrix products: 31.4 us -> none  [the longest x6 22.3 us: product(): jnp.dot(left, right, precision=exact_mode, preferred_element_type=jnp.flo...]
    ppermute x12 -> x0, starting transfers between devices: 29.7 us -> none  [the longest x8 24.4 us: passed_along(): return lax.ppermute(block, axis, route)]
    all_to_all x3 -> x0, starting transfers between devices: 27 us -> none  [the longest x1 11.9 us: coarse_level(): lax.all_to_all(outgoing_rows, ('blk', 'lat'), split_axis=0, concat_axis=0...]
    unnamed x36 -> x13, local copies, waits for them, and re-layouts: 26.8 us -> 5.68 us
    reduce_sum x5 -> x0, other arithmetic: 10.3 us -> none  [the longest x1 3.92 us: shards(): jnp.sum(new_residual * new_residual, axis=0)]
  transfers between devices with their start and end apart: 15 -> 0, of which waited for: 4 -> 0; matrix products, arithmetic and copies ran while one was open for 10% -> 0% of each run, Pallas kernels for 0% -> 0%
where the time goes in v1:
time: 131 us
  Pallas kernels  125 us (95%)
  local copies, waits for them, and re-layouts  5.68 us (4%)
    pallas_call x1, Pallas kernels, shards(): pl.pallas_call(functools.partial(step_kernel, sizes, norm_scale), out_sha...  125 us
    unnamed x13, local copies, waits for them, and re-layouts  5.68 us

profile of v1, /device:TPU:1, one launch (start us, length us, event | category | flops | bytes accessed | tf_op | source)
XLA Modules:
  0.0 130.9 jit_solution(7496084892919638360)
XLA Ops:
  0.6 124.6 %shard_map.137 = (f32[768,512]{1,0:T(8,128)}, f32[768,512]{1,0:T(8,128)}, f32[1,512]{1,0:T(1,128)}, f32[1,512]{1,0:T(1,128)}, f32[1,512]{1,0:T(1,128)}) custom-call(s32[6]{0:T(128)} %bitcast.29, s32[1,256]{1,0:T(1,128)} %bitcast.27, s32[1,256]{1,0:T(1,128)} %bitcast.28, f32[1,512]{1,0:T(1,128)} %bitcast.26, f32[768,512]{1,0:T(8,128)} %bitcast.19, ...), custom_call_target="tpu_custom_call" | custom-call | tf_op jit(solution)/shard_map/pallas_call | solution.py:543
  125.2 0.0 copy-start
  125.2 2.8 %copy.20 = f32[1,1,1,768,512]{4,3,2,1,0:T(8,128)} copy(f32[1,1,1,768,512]{4,3,2,1,0:T(8,128)} %bitcast.18) | data formatting | bytes 3145728
  128.0 0.0 copy-done
  128.0 0.0 copy-start.3
  128.0 0.0 copy-start.2
  128.0 0.0 copy-start.1
  128.0 1.1 copy.21
  129.2 0.0 copy-done.3
  129.2 0.6 copy.22
  129.7 0.0 copy-done.2
  129.7 0.6 copy.23
  130.3 0.0 copy-done.1
  130.3 0.6 copy.24
Async XLA Ops:
  125.2 2.8 %copy-start = (f32[768,512]{1,0:T(8,128)S(1)}, f32[768,512]{1,0:T(8,128)}, u32[]{:S(2)}) copy-start(f32[768,512]{1,0:T(8,128)} %get-tuple-element.11) | copy-start | bytes 4718596
  128.0 1.2 copy-start.3
  128.0 1.7 %copy-start.2 = (f32[1,512]{1,0:T(1,128)S(1)}, f32[1,512]{1,0:T(1,128)}, u32[]{:S(2)}) copy-start(f32[1,512]{1,0:T(1,128)} %get-tuple-element.13) | copy-start | bytes 6148
  128.0 2.3 %copy-start.1 = (f32[1,512]{1,0:T(1,128)S(1)}, f32[1,512]{1,0:T(1,128)}, u32[]{:S(2)}) copy-start(f32[1,512]{1,0:T(1,128)} %get-tuple-element.14) | copy-start | bytes 6148

commit v2 on v1

--- a/solution.py
+++ b/solution.py
@@ -46,9 +46,7 @@
     c_hbm,
     nr_hbm,
     dir_hbm,
-    rho_ref,
-    alpha_ref,
-    norm_ref,
+    small_ref,
     r_v,
     pp_v,
     s_v,
@@ -59,6 +57,8 @@
     wl_v,
     th_v,
     tl_v,
+    pth_v,
+    ptl_v,
     slotr_v,
     slotc_v,
     pick_v,
@@ -67,10 +67,8 @@
     rows_in,
     out_buf,
     in_buf,
-    rel1,
     ans_buf,
     ret_buf,
-    rel2,
     gath_v,
     nloc_v,
     img_v,
@@ -87,16 +85,12 @@
     row_r,
     x_s,
     x_r,
-    rel_s,
-    rel_r,
-    fwd_s,
     ara_s,
     ara_r,
     arb_s,
     arb_r,
     f_s,
     f_r,
-    own_sem,
     o_sem,
 ):
     n_blk, n_lat, n_depth = sizes
@@ -108,7 +102,6 @@
     nc = phi_v.shape[1]
     co = c_v.shape[0]
     half = n_blk // 2
-    quarter = n_blk // 4
 
     def load(src, dst, k):
         return pltpu.make_async_copy(src, dst, ld_sem.at[k])
@@ -124,7 +117,10 @@
     for one in loads:
         one.start()
 
-    in_buf[:, CAP:, :] = jnp.zeros((owners, STRIDE - CAP, nr), F32)
+    hw = nr // 2
+    cols = (pl.ds(0, hw), pl.ds(hw, hw))
+    for h in range(2):
+        in_buf[h, :, CAP:, :] = jnp.zeros((owners, STRIDE - CAP, hw), F32)
 
     def peer(k):
         db, j = k // n_lat, k % n_lat
@@ -178,10 +174,19 @@
         wh_v[rows, :] = wh
         wl_v[rows, :] = wl
     loads[1].wait()
-    terms = mm3(jnp.transpose(phi_v[...]), wh_v[...], wl_v[...])
-    th, tl = split(terms)
-    th_v[...] = th
-    tl_v[...] = tl
+    ph, plo = split(jnp.transpose(phi_v[...]))
+    pth_v[...] = ph
+    ptl_v[...] = plo
+
+    def coarse_terms(h):
+        c = cols[h]
+        wh, wl = wh_v[:, c], wl_v[:, c]
+        terms = mm(pth_v[...], wh) + (mm(pth_v[...], wl) + mm(ptl_v[...], wh))
+        th, tl = split(terms)
+        th_v[:, c] = th
+        tl_v[:, c] = tl
+
+    coarse_terms(0)
 
     pl.semaphore_wait(barrier, owners - 1 + n_depth - 1)
 
@@ -200,71 +205,52 @@
     lax.fori_loop(1, owners, rows_copy, 0)
     pltpu.make_async_copy(rows_out.at[me], rows_in.at[me], row_r.at[0]).start()
 
-    def tile_copy(src, dst, way, dev):
-        return pltpu.make_async_remote_copy(
-            src_ref=src,
-            dst_ref=dst,
-            send_sem=x_s.at[way],
-            recv_sem=x_r.at[way],
-            device_id=dev,
-            device_id_type=MESH,
-        )
-
-    def tile_sends(src_of, dst_of, rel, way, db):
+    def tile_sends(src_of, dst_of, way, h, db):
         tb = lax.rem(b + db, n_blk)
         for j in range(n_lat):
             tl_ = lax.rem(l + j, n_lat)
-            src = src_of(tb * n_lat + tl_)
-            if db == half:
-                via = quarter if j < n_lat // 2 else n_blk - quarter
+            src = src_of(h, tb * n_lat + tl_)
+            if db == 0 and j == 0:
+                pltpu.make_async_copy(src, dst_of(h, me), x_r.at[way, h]).start()
+            else:
                 pltpu.make_async_remote_copy(
                     src_ref=src,
-                    dst_ref=rel.at[j],
-                    send_sem=rel_s.at[way],
-                    recv_sem=rel_r.at[way],
-                    device_id=(lax.rem(b + via, n_blk), l, d),
+                    dst_ref=dst_of(h, me),
+                    send_sem=x_s.at[way, h],
+                    recv_sem=x_r.at[way, h],
+                    device_id=(tb, tl_, d),
                     device_id_type=MESH,
                 ).start()
-            elif db == 0 and j == 0:
-                pltpu.make_async_copy(src, dst_of(me), x_r.at[way]).start()
-            else:
-                tile_copy(src, dst_of(me), way, (tb, tl_, d)).start()
-
-    def tile_forward(dst_of, rel, way):
-        pltpu.make_async_copy(rel, rel, rel_r.at[way]).wait()
-        for j in range(n_lat):
-            go = quarter if j < n_lat // 2 else n_blk - quarter
-            origin = lax.rem(b + n_blk - go, n_blk) * n_lat + l
-            pltpu.make_async_remote_copy(
-                src_ref=rel.at[j],
-                dst_ref=dst_of(origin),
-                send_sem=fwd_s.at[way],
-                recv_sem=x_r.at[way],
-                device_id=(lax.rem(b + go, n_blk), lax.rem(l + j, n_lat), d),
-                device_id_type=MESH,
-            ).start()
+
+    def tile_wait(dst_of, way, h):
+        got = dst_of(h, slice(None))
+        pltpu.make_async_copy(got, got, x_r.at[way, h]).wait()
 
     order = [half]
     for step in range(half - 1, 0, -1):
         order += [step, n_blk - step]
     order += [0]
 
-    out_of = lambda o: out_buf.at[o]
-    in_of = lambda o: in_buf.at[o, pl.ds(0, CAP)]
-    ans_of = lambda o: ans_buf.at[o, pl.ds(0, CAP)]
-    ret_of = lambda o: ret_buf.at[o]
+    out_of = lambda h, o: out_buf.at[h, o]
+    in_of = lambda h, o: in_buf.at[h, o, pl.ds(0, CAP)]
+    ans_of = lambda h, o: ans_buf.at[h, o, pl.ds(0, CAP)]
+    ret_of = lambda h, o: ret_buf.at[h, o]
 
     chunk = n_lat * CAP
-    for db in order:
-        tb = lax.rem(b + db, n_blk)
-        pack = jnp.where(
-            iota((chunk, nc), 0) + tb * chunk == jnp.broadcast_to(slotr_v[...], (chunk, nc)),
-            1.0,
-            0.0,
-        ).astype(BF16)
-        tiles = mm(pack, th_v[...]) + mm(pack, tl_v[...])
-        out_buf[pl.ds(tb * n_lat, n_lat)] = tiles.reshape(n_lat, CAP, nr)
-        tile_sends(out_of, in_of, rel1, 0, db)
+    for h in range(2):
+        c = cols[h]
+        if h:
+            coarse_terms(h)
+        for db in order:
+            tb = lax.rem(b + db, n_blk)
+            pack = jnp.where(
+                iota((chunk, nc), 0) + tb * chunk == jnp.broadcast_to(slotr_v[...], (chunk, nc)),
+                1.0,
+                0.0,
+            ).astype(BF16)
+            tiles = mm(pack, th_v[:, c]) + mm(pack, tl_v[:, c])
+            out_buf[h, pl.ds(tb * n_lat, n_lat)] = tiles.reshape(n_lat, CAP, hw)
+            tile_sends(out_of, in_of, 0, h, db)
 
     loads[2].wait()
 
@@ -274,10 +260,7 @@
         nloc_v[rows, :] = y
         return acc + jnp.sum(r_v[rows, :] * y, axis=0, keepdims=True)
 
-    rho_local = lax.fori_loop(0, 3, local_block, jnp.zeros((1, nr), F32))
-    tile_forward(in_of, rel1, 0)
-    rho_local = lax.fori_loop(3, 6, local_block, rho_local)
-    ar_src[0] = rho_local
+    ar_src[0] = lax.fori_loop(0, 6, local_block, jnp.zeros((1, nr), F32))
 
     pltpu.make_async_copy(rows_in, rows_in, row_r.at[0]).wait()
     wide = n_lat * STRIDE
@@ -296,24 +279,6 @@
             ).astype(BF16)
     loads[3].wait()
 
-    pltpu.make_async_copy(in_of(slice(None)), in_of(slice(None)), x_r.at[0]).wait()
-    per = 2 * n_lat
-    for g in range(n_blk // 2):
-        xh, xl = split(in_buf[pl.ds(g * per, per)].reshape(per * STRIDE, nr))
-        pick = pick_v[:, pl.ds(g * 2 * wide, 2 * wide)]
-        part = mm(pick, xh) + mm(pick, xl)
-        if g == 0:
-            gath_v[...] = part
-        else:
-            gath_v[...] += part
-    gathered = gath_v[...]
-    gh, gl = split(gathered)
-    solved = mm3(c_v[...], gh, gl)
-    ar_src[0] += 2.0 * jnp.sum(gathered * solved, axis=0, keepdims=True)
-    sh, sl = split(solved)
-    th_v[...] = sh
-    tl_v[...] = sl
-
     def reduce_start(k):
         def send(i, c):
             pb, plat = peer(i)
@@ -352,85 +317,115 @@
         pltpu.make_async_copy(ar_b.at[k], ar_b.at[k], arb_r.at[k]).wait()
         return jnp.sum(ar_b[k], axis=0)
 
-    reduce_start(0)
-    for db in order:
-        tb = lax.rem(b + db, n_blk)
-        pick = pickt_v[tb]
-        tiles = mm(pick, th_v[...]) + mm(pick, tl_v[...])
-        ans_buf[pl.ds(tb * n_lat, n_lat)] = tiles.reshape(n_lat, STRIDE, nr)
-        tile_sends(ans_of, ret_of, rel2, 1, db)
-    tile_forward(ret_of, rel2, 1)
+    per = 2 * n_lat
+    for h in range(2):
+        c = cols[h]
+        tile_wait(in_of, 0, h)
+        for g in range(n_blk // 2):
+            xh, xl = split(in_buf[h, pl.ds(g * per, per)].reshape(per * STRIDE, hw))
+            pick = pick_v[:, pl.ds(g * 2 * wide, 2 * wide)]
+            part = mm(pick, xh) + mm(pick, xl)
+            if g == 0:
+                gath_v[:, c] = part
+            else:
+                gath_v[:, c] += part
+        gathered = gath_v[:, c]
+        gh, gl = split(gathered)
+        solved = mm3(c_v[...], gh, gl)
+        ar_src[0, :, c] += 2.0 * jnp.sum(gathered * solved, axis=0, keepdims=True)
+        sh, sl = split(solved)
+        th_v[:, c] = sh
+        tl_v[:, c] = sl
+        if h:
+            reduce_start(0)
+        for db in order:
+            tb = lax.rem(b + db, n_blk)
+            pick = pickt_v[tb]
+            tiles = mm(pick, th_v[:, c]) + mm(pick, tl_v[:, c])
+            ans_buf[h, pl.ds(tb * n_lat, n_lat)] = tiles.reshape(n_lat, STRIDE, hw)
+            tile_sends(ans_of, ret_of, 1, h, db)
     reduce_middle(0)
     rho_now = norm_scale * reduce_end(0)
-    rho_ref[...] = rho_now
+    small_ref[0] = rho_now
     beta = rho_now / prho_ref[...]
     loads[4].wait()
     loads[5].wait()
 
-    pltpu.make_async_copy(ret_buf, ret_buf, x_r.at[1]).wait()
-    lanes = 8 * CAP
-    for g in range(owners // 8):
-        yh, yl = split(ret_buf[pl.ds(g * 8, 8)].reshape(lanes, nr))
-        pack_t = jnp.where(slotc_v[:, :lanes] == iota((nc, lanes), 1) + g * lanes, 1.0, 0.0).astype(BF16)
-        part = mm(pack_t, yh) + mm(pack_t, yl)
-        if g == 0:
-            gath_v[...] = part
-        else:
-            gath_v[...] += part
-    ch, cl = split(gath_v[...])
-    th_v[...] = ch
-    tl_v[...] = cl
-
-    def face_send(src, rx, turn, f):
+    def face_copy(src, rx, f, c, ssem, rsem):
         step = 1 if f % 2 == 1 else -1
         axis = f // 2
         dev = [b, l, d]
         n = sizes[axis]
         dev[axis] = lax.rem(dev[axis] + n + step, n)
         return pltpu.make_async_remote_copy(
-            src_ref=src.at[pl.ds(f * face, face)],
-            dst_ref=rx.at[f ^ 1],
-            send_sem=f_s.at[turn, f],
-            recv_sem=f_r.at[turn, f ^ 1],
+            src_ref=src.at[pl.ds(f * face, face), c],
+            dst_ref=rx.at[f ^ 1, :, c],
+            send_sem=ssem.at[f],
+            recv_sem=rsem.at[f ^ 1],
             device_id=tuple(dev),
             device_id_type=MESH,
         )
 
-    for f in range(6):
-        rows = pl.ds(f * face, face)
-        img_v[rows, :] = nloc_v[rows, :] + mm3(phi_v[rows, :], th_v[...], tl_v[...])
-        face_send(img_v, rx1, 0, f).start()
-
-    for f in (4, 5, 2, 3, 0, 1):
-        rows = pl.ds(f * face, face)
-        face_send(img_v, rx1, 0, f ^ 1).wait_recv()
-        live = iota((face, nr), 0) < fl_ref[f]
-        p = jnp.where(live, 0.5 * (img_v[rows, :] + rx1[f]) + beta * pp_v[rows, :], 0.0)
-        p_v[rows, :] = p
-        ph, plo = split(p)
-        wh_v[rows, :] = ph
-        wl_v[rows, :] = plo
+    def image_face(h, f):
+        return face_copy(img_v, rx1, f, cols[h], f_s.at[h], f_r.at[h])
+
+    def schur_face(f):
+        return face_copy(simg_v, rx2, f, pl.ds(0, nr), f_s.at[2], f_r.at[2])
+
+    lanes = 8 * CAP
+    for h in range(2):
+        c = cols[h]
+        tile_wait(ret_of, 1, h)
+        for g in range(owners // 8):
+            yh, yl = split(ret_buf[h, pl.ds(g * 8, 8)].reshape(lanes, hw))
+            pack_t = jnp.where(
+                slotc_v[:, :lanes] == iota((nc, lanes), 1) + g * lanes, 1.0, 0.0
+            ).astype(BF16)
+            part = mm(pack_t, yh) + mm(pack_t, yl)
+            if g == 0:
+                gath_v[:, c] = part
+            else:
+                gath_v[:, c] += part
+        ch, cl = split(gath_v[:, c])
+        for f in range(6):
+            rows = pl.ds(f * face, face)
+            img_v[rows, c] = nloc_v[rows, c] + mm3(phi_v[rows, :], ch, cl)
+            image_face(h, f).start()
+
+    for h in range(2):
+        c = cols[h]
+        for f in (4, 5, 2, 3, 0, 1):
+            rows = pl.ds(f * face, face)
+            image_face(h, f ^ 1).wait_recv()
+            live = iota((face, hw), 0) < fl_ref[f]
+            p = jnp.where(
+                live, 0.5 * (img_v[rows, c] + rx1[f, :, c]) + beta[:, h * hw : (h + 1) * hw] * pp_v[rows, c], 0.0
+            )
+            p_v[rows, c] = p
+            ph, plo = split(p)
+            wh_v[rows, c] = ph
+            wl_v[rows, c] = plo
+
+        def schur_block(f, acc):
+            rows = pl.ds(pl.multiple_of(f * face, face), face)
+            y = mm3(s_v[rows, :], wh_v[:, c], wl_v[:, c])
+            simg_v[rows, c] = y
+            return acc + jnp.sum(p_v[rows, c] * y, axis=0, keepdims=True)
+
+        ar_src[1, :, c] = lax.fori_loop(0, 6, schur_block, jnp.zeros((1, hw), F32))
     dir_out = pltpu.make_async_copy(p_v, dir_hbm, o_sem.at[0])
     dir_out.start()
-
-    def schur_block(f, acc):
-        rows = pl.ds(pl.multiple_of(f * face, face), face)
-        y = mm3(s_v[rows, :], wh_v[...], wl_v[...])
-        simg_v[rows, :] = y
-        return acc + jnp.sum(p_v[rows, :] * y, axis=0, keepdims=True)
-
-    ar_src[1] = lax.fori_loop(0, 6, schur_block, jnp.zeros((1, nr), F32))
     reduce_start(1)
     for f in range(6):
-        face_send(simg_v, rx2, 1, f).start()
+        schur_face(f).start()
     reduce_middle(1)
     alpha = rho_now / (norm_scale * (2.0 * reduce_end(1)))
-    alpha_ref[...] = alpha
+    small_ref[1] = alpha
 
     total = jnp.zeros((1, nr), F32)
     for f in (4, 5, 2, 3, 0, 1):
         rows = pl.ds(f * face, face)
-        face_send(simg_v, rx2, 1, f ^ 1).wait_recv()
+        schur_face(f ^ 1).wait_recv()
         live = iota((face, nr), 0) < fl_ref[f]
         q = r_v[rows, :] - alpha * jnp.where(live, simg_v[rows, :] + rx2[f], 0.0)
         nloc_v[rows, :] = q
@@ -440,7 +435,7 @@
     nr_out = pltpu.make_async_copy(nloc_v, nr_hbm, o_sem.at[1])
     nr_out.start()
     reduce_middle(2)
-    norm_ref[...] = norm_scale * reduce_end(2)
+    small_ref[2] = norm_scale * reduce_end(2)
 
     dir_out.wait()
     nr_out.wait()
@@ -450,18 +445,37 @@
         pltpu.make_async_copy(src, src, sem).wait()
 
     left(rows_out.at[most], row_s.at[0])
-    direct = pl.ds(0, owners - 1 - n_lat)
-    left(out_buf.at[direct], x_s.at[0])
-    left(out_buf.at[direct], x_s.at[1])
-    for way, rel in ((0, rel1), (1, rel2)):
-        left(rel, rel_s.at[way])
-        left(rel, fwd_s.at[way])
+    for way in range(2):
+        for h in range(2):
+            left(out_buf.at[h, most], x_s.at[way, h])
     for k in range(3):
         left(ar_a.at[k, most], ara_s.at[k])
         left(ar_b.at[k, pl.ds(0, n_depth - 1)], arb_s.at[k])
-    for turn, src, rx in ((0, img_v, rx1), (1, simg_v, rx2)):
-        for f in range(6):
-            face_send(src, rx, turn, f).wait_send()
+    for f in range(6):
+        image_face(0, f).wait_send()
+        image_face(1, f).wait_send()
+        schur_face(f).wait_send()
+
+
+def pass_kernel(q_hbm, p_hbm, small, nr_hbm, dir_hbm, rho_ref, alpha_ref, norm_ref, q_v, p_v, sems):
+    parts = 4
+    rows = q_v.shape[0] // parts
+    ins, outs = [], []
+    for k, (src, mid, dst) in enumerate(((p_hbm, p_v, dir_hbm), (q_hbm, q_v, nr_hbm))):
+        for i in range(parts):
+            at = pl.ds(i * rows, rows)
+            ins.append(pltpu.make_async_copy(src.at[at], mid.at[at], sems.at[0, k, i]))
+            outs.append(pltpu.make_async_copy(mid.at[at], dst.at[at], sems.at[1, k, i]))
+    for one in ins:
+        one.start()
+    rho_ref[...] = small[0]
+    alpha_ref[...] = small[1]
+    norm_ref[...] = small[2]
+    for got, out in zip(ins, outs):
+        got.wait()
+        out.start()
+    for out in outs:
+        out.wait()
 
 
 def shards(
@@ -500,18 +514,18 @@
         vm((nb, nr), BF16),
         vm((nc, nr), BF16),
         vm((nc, nr), BF16),
+        vm((nc, nb), BF16),
+        vm((nc, nb), BF16),
         vm((1, nc), jnp.int32),
         vm((nc, nc), jnp.int32),
         vm((co, owners * STRIDE), BF16),
         vm((sizes[0], sizes[1] * STRIDE, co), BF16),
         vm((owners, 1, 4 * STRIDE), F32),
         vm((owners, 1, 4 * STRIDE), F32),
-        vm((owners, CAP, nr), F32),
-        vm((owners, STRIDE, nr), F32),
-        vm((sizes[1], CAP, nr), F32),
-        vm((owners, STRIDE, nr), F32),
-        vm((owners, CAP, nr), F32),
-        vm((sizes[1], CAP, nr), F32),
+        vm((2, owners, CAP, nr // 2), F32),
+        vm((2, owners, STRIDE, nr // 2), F32),
+        vm((2, owners, STRIDE, nr // 2), F32),
+        vm((2, owners, CAP, nr // 2), F32),
         vm((nc, nr), F32),
         vm((nb, nr), F32),
         vm((nb, nr), F32),
@@ -526,25 +540,21 @@
         sem((6,)),
         sem((1,)),
         sem((1,)),
-        sem((2,)),
-        sem((2,)),
-        sem((2,)),
-        sem((2,)),
-        sem((2,)),
+        sem((2, 2)),
+        sem((2, 2)),
         sem((3,)),
         sem((3,)),
         sem((3,)),
         sem((3,)),
-        sem((2, 6)),
-        sem((2, 6)),
-        sem((1,)),
+        sem((3, 6)),
+        sem((3, 6)),
         sem((2,)),
     ]
-    new_residual, direction, rho_now, step_alpha, res_norm = pl.pallas_call(
+    q, p, totals = pl.pallas_call(
         functools.partial(step_kernel, sizes, norm_scale),
-        out_shape=(big, big, small, small, small),
+        out_shape=(big, big, jax.ShapeDtypeStruct((3, 1, nr), F32)),
         in_specs=[pl.BlockSpec(memory_space=pltpu.SMEM), whole, whole, whole] + [far] * 6,
-        out_specs=(far, far, whole, whole, whole),
+        out_specs=(far, far, whole),
         scratch_shapes=scratch,
         compiler_params=pltpu.CompilerParams(
             collective_id=0, has_side_effects=True, vmem_limit_bytes=60 * 1024 * 1024
@@ -561,6 +571,13 @@
         coarse_basis.reshape(nb, nc),
         coarse_inverse.reshape(co, co),
     )
+    new_residual, direction, rho_now, step_alpha, res_norm = pl.pallas_call(
+        pass_kernel,
+        out_shape=(big, big, small, small, small),
+        in_specs=[far, far, whole],
+        out_specs=(far, far, whole, whole, whole),
+        scratch_shapes=[vm((nb, nr), F32), vm((nb, nr), F32), sem((2, 2, 4))],
+    )(q, p, totals)
     out_shape = (1, 1, 1, nb, nr)
     return (
         new_residual.reshape(out_shape),

time: 131 us -> 121 us (0.924)
  local copies, waits for them, and re-layouts: 5.68 us -> 0 us
  Pallas kernels: 125 us -> 120 us
    pallas_call x1, Pallas kernels: 125 us -> 116 us  [shards(): pl.pallas_call(functools.partial(step_kernel, sizes, norm_scale), out_sha...]
    unnamed x13 -> x0, local copies, waits for them, and re-layouts: 5.68 us -> none
    pallas_call x0 -> x1, Pallas kernels: none -> 4.06 us  [shards(): pl.pallas_call(pass_kernel, out_shape=(big, big, small, small, small), in...]
where the time goes in v2:
time: 121 us; the launch traced here: 120 us
  Pallas kernels  120 us (99%)
    pallas_call x1, Pallas kernels, shards(): pl.pallas_call(functools.partial(step_kernel, sizes, norm_scale), out_sha...  116 us
    pallas_call x1, Pallas kernels, shards(): pl.pallas_call(pass_kernel, out_shape=(big, big, small, small, small), in...  4.06 us

profile of v2, /device:TPU:1, one launch (start us, length us, event | category | flops | bytes accessed | tf_op | source)
XLA Modules:
  0.0 120.4 jit_solution(5611236861235100209)
XLA Ops:
  0.6 115.7 %shard_map.137 = (f32[768,512]{1,0:T(8,128)}, f32[768,512]{1,0:T(8,128)}, f32[3,1,512]{2,1,0:T(1,128)}) custom-call(s32[6]{0:T(128)} %bitcast.24, s32[1,256]{1,0:T(1,128)} %bitcast.22, s32[1,256]{1,0:T(1,128)} %bitcast.23, f32[1,512]{1,0:T(1,128)} %bitcast.21, f32[768,512]{1,0:T(8,128)} %bitcast.17, f32[768,512]{1,0:T(8,128)} %bitcast.18, ...), custom_call_target="tpu_custom_call" | custom-call | tf_op jit(solution)/shard_map/pallas_call | solution.py:553
  116.3 4.1 %shard_map.138 = (f32[768,512]{1,0:T(8,128)}, f32[768,512]{1,0:T(8,128)}, f32[1,512]{1,0:T(1,128)}, f32[1,512]{1,0:T(1,128)}, f32[1,512]{1,0:T(1,128)}) custom-call(f32[768,512]{1,0:T(8,128)} %get-tuple-element.13.q_hbm, f32[768,512]{1,0:T(8,128)} %get-tuple-element.14.p_hbm, f32[3,1,512]{2,1,0:T(1,128)} %get-tuple-element.15.small), custom_call_target="tpu_custom_call" | custom-call | tf_op jit(solution)/shard_map/pallas_call | solution.py:574

commit v3 on v2

--- a/solution.py
+++ b/solution.py
@@ -8,6 +8,9 @@
 
 CAP = 24
 STRIDE = 32
+PARTS = 4
+CUTS = (0, 2, 4)
+GROUPS = ((0, 2), (2, 4))
 F32 = jnp.float32
 BF16 = jnp.bfloat16
 MESH = pl.DeviceIdType.MESH
@@ -101,7 +104,6 @@
     face = nb // 6
     nc = phi_v.shape[1]
     co = c_v.shape[0]
-    half = n_blk // 2
 
     def load(src, dst, k):
         return pltpu.make_async_copy(src, dst, ld_sem.at[k])
@@ -117,31 +119,28 @@
     for one in loads:
         one.start()
 
-    hw = nr // 2
-    cols = (pl.ds(0, hw), pl.ds(hw, hw))
-    for h in range(2):
-        in_buf[h, :, CAP:, :] = jnp.zeros((owners, STRIDE - CAP, hw), F32)
-
-    def peer(k):
-        db, j = k // n_lat, k % n_lat
-        return lax.rem(b + db, n_blk), lax.rem(l + j, n_lat)
+    part_w = nr // PARTS
+    chunks = len(CUTS) - 1
+    widths = [(CUTS[h + 1] - CUTS[h]) * part_w for h in range(chunks)]
+    cols = [pl.ds(CUTS[h] * part_w, widths[h]) for h in range(chunks)]
+    in_buf[:, CAP:, :] = jnp.zeros((owners, STRIDE - CAP, nr), F32)
+
+    at_blk = [b] + [lax.rem(b + k, n_blk) for k in range(1, n_blk)]
+    at_lat = [l] + [lax.rem(l + k, n_lat) for k in range(1, n_lat)]
+    at_depth = [d] + [lax.rem(d + k, n_depth) for k in range(1, n_depth)]
+
+    def far_first(n):
+        return sorted(range(n), key=lambda k: -min(k, n - k))
+
+    order = far_first(n_blk)
+    layer = [
+        (at_blk[i], at_lat[j], d) for i in order for j in far_first(n_lat) if i or j
+    ]
+    column = [(b, l, at_depth[k]) for k in range(1, n_depth)]
 
     barrier = pltpu.get_barrier_semaphore()
-
-    def greet(k, c):
-        pb, plat = peer(k)
-        pl.semaphore_signal(barrier, inc=1, device_id=(pb, plat, d), device_id_type=MESH)
-        return c
-
-    lax.fori_loop(1, owners, greet, 0)
-
-    def greet_depth(k, c):
-        pl.semaphore_signal(
-            barrier, inc=1, device_id=(b, l, lax.rem(d + k, n_depth)), device_id_type=MESH
-        )
-        return c
-
-    lax.fori_loop(1, n_depth, greet_depth, 0)
+    for dev in layer + column:
+        pl.semaphore_signal(barrier, inc=1, device_id=dev, device_id_type=MESH)
 
     own_row = own_ref[...]
     own_b = jnp.broadcast_to(own_row.astype(F32), (nc, nc))
@@ -190,25 +189,21 @@
 
     pl.semaphore_wait(barrier, owners - 1 + n_depth - 1)
 
-    def rows_copy(k, c):
-        pb, plat = peer(k)
+    for dev in layer:
         pltpu.make_async_remote_copy(
-            src_ref=rows_out.at[pb * n_lat + plat],
+            src_ref=rows_out.at[dev[0] * n_lat + dev[1]],
             dst_ref=rows_in.at[me],
             send_sem=row_s.at[0],
             recv_sem=row_r.at[0],
-            device_id=(pb, plat, d),
+            device_id=dev,
             device_id_type=MESH,
         ).start()
-        return c
-
-    lax.fori_loop(1, owners, rows_copy, 0)
     pltpu.make_async_copy(rows_out.at[me], rows_in.at[me], row_r.at[0]).start()
 
     def tile_sends(src_of, dst_of, way, h, db):
-        tb = lax.rem(b + db, n_blk)
+        tb = at_blk[db]
         for j in range(n_lat):
-            tl_ = lax.rem(l + j, n_lat)
+            tl_ = at_lat[j]
             src = src_of(h, tb * n_lat + tl_)
             if db == 0 and j == 0:
                 pltpu.make_async_copy(src, dst_of(h, me), x_r.at[way, h]).start()
@@ -226,30 +221,25 @@
         got = dst_of(h, slice(None))
         pltpu.make_async_copy(got, got, x_r.at[way, h]).wait()
 
-    order = [half]
-    for step in range(half - 1, 0, -1):
-        order += [step, n_blk - step]
-    order += [0]
-
-    out_of = lambda h, o: out_buf.at[h, o]
-    in_of = lambda h, o: in_buf.at[h, o, pl.ds(0, CAP)]
-    ans_of = lambda h, o: ans_buf.at[h, o, pl.ds(0, CAP)]
-    ret_of = lambda h, o: ret_buf.at[h, o]
+    out_of = lambda h, o: out_buf.at[o, :, cols[h]]
+    in_of = lambda h, o: in_buf.at[o, pl.ds(0, CAP), cols[h]]
+    ans_of = lambda h, o: ans_buf.at[o, pl.ds(0, CAP), cols[h]]
+    ret_of = lambda h, o: ret_buf.at[o, :, cols[h]]
 
     chunk = n_lat * CAP
-    for h in range(2):
-        c = cols[h]
+    for h in range(chunks):
+        c, hw = cols[h], widths[h]
         if h:
             coarse_terms(h)
         for db in order:
-            tb = lax.rem(b + db, n_blk)
+            tb = at_blk[db]
             pack = jnp.where(
                 iota((chunk, nc), 0) + tb * chunk == jnp.broadcast_to(slotr_v[...], (chunk, nc)),
                 1.0,
                 0.0,
             ).astype(BF16)
             tiles = mm(pack, th_v[:, c]) + mm(pack, tl_v[:, c])
-            out_buf[h, pl.ds(tb * n_lat, n_lat)] = tiles.reshape(n_lat, CAP, hw)
+            out_buf[pl.ds(tb * n_lat, n_lat), :, c] = tiles.reshape(n_lat, CAP, hw)
             tile_sends(out_of, in_of, 0, h, db)
 
     loads[2].wait()
@@ -280,37 +270,30 @@
     loads[3].wait()
 
     def reduce_start(k):
-        def send(i, c):
-            pb, plat = peer(i)
+        for dev in layer:
             pltpu.make_async_remote_copy(
                 src_ref=ar_src.at[k],
                 dst_ref=ar_a.at[k, me],
                 send_sem=ara_s.at[k],
                 recv_sem=ara_r.at[k],
-                device_id=(pb, plat, d),
+                device_id=dev,
                 device_id_type=MESH,
             ).start()
-            return c
-
-        lax.fori_loop(1, owners, send, 0)
         pltpu.make_async_copy(ar_src.at[k], ar_a.at[k, me], ara_r.at[k]).start()
 
     def reduce_middle(k):
         pltpu.make_async_copy(ar_a.at[k], ar_a.at[k], ara_r.at[k]).wait()
         ar_mid[k] = jnp.sum(ar_a[k], axis=0)
 
-        def send(i, c):
+        for dev in column:
             pltpu.make_async_remote_copy(
                 src_ref=ar_mid.at[k],
                 dst_ref=ar_b.at[k, d],
                 send_sem=arb_s.at[k],
                 recv_sem=arb_r.at[k],
-                device_id=(b, l, lax.rem(d + i, n_depth)),
+                device_id=dev,
                 device_id_type=MESH,
             ).start()
-            return c
-
-        lax.fori_loop(1, n_depth, send, 0)
         pltpu.make_async_copy(ar_mid.at[k], ar_b.at[k, d], arb_r.at[k]).start()
 
     def reduce_end(k):
@@ -318,11 +301,11 @@
         return jnp.sum(ar_b[k], axis=0)
 
     per = 2 * n_lat
-    for h in range(2):
-        c = cols[h]
+    for h in range(chunks):
+        c, hw = cols[h], widths[h]
         tile_wait(in_of, 0, h)
         for g in range(n_blk // 2):
-            xh, xl = split(in_buf[h, pl.ds(g * per, per)].reshape(per * STRIDE, hw))
+            xh, xl = split(in_buf[pl.ds(g * per, per), :, c].reshape(per * STRIDE, hw))
             pick = pick_v[:, pl.ds(g * 2 * wide, 2 * wide)]
             part = mm(pick, xh) + mm(pick, xl)
             if g == 0:
@@ -336,13 +319,13 @@
         sh, sl = split(solved)
         th_v[:, c] = sh
         tl_v[:, c] = sl
-        if h:
+        if h == chunks - 1:
             reduce_start(0)
         for db in order:
-            tb = lax.rem(b + db, n_blk)
+            tb = at_blk[db]
             pick = pickt_v[tb]
             tiles = mm(pick, th_v[:, c]) + mm(pick, tl_v[:, c])
-            ans_buf[h, pl.ds(tb * n_lat, n_lat)] = tiles.reshape(n_lat, STRIDE, hw)
+            ans_buf[pl.ds(tb * n_lat, n_lat), :, c] = tiles.reshape(n_lat, STRIDE, hw)
             tile_sends(ans_of, ret_of, 1, h, db)
     reduce_middle(0)
     rho_now = norm_scale * reduce_end(0)
@@ -370,14 +353,14 @@
         return face_copy(img_v, rx1, f, cols[h], f_s.at[h], f_r.at[h])
 
     def schur_face(f):
-        return face_copy(simg_v, rx2, f, pl.ds(0, nr), f_s.at[2], f_r.at[2])
+        return face_copy(simg_v, rx2, f, pl.ds(0, nr), f_s.at[chunks], f_r.at[chunks])
 
     lanes = 8 * CAP
-    for h in range(2):
-        c = cols[h]
+    for h in range(chunks):
+        c, hw = cols[h], widths[h]
         tile_wait(ret_of, 1, h)
         for g in range(owners // 8):
-            yh, yl = split(ret_buf[h, pl.ds(g * 8, 8)].reshape(lanes, hw))
+            yh, yl = split(ret_buf[pl.ds(g * 8, 8), :, c].reshape(lanes, hw))
             pack_t = jnp.where(
                 slotc_v[:, :lanes] == iota((nc, lanes), 1) + g * lanes, 1.0, 0.0
             ).astype(BF16)
@@ -392,42 +375,54 @@
             img_v[rows, c] = nloc_v[rows, c] + mm3(phi_v[rows, :], ch, cl)
             image_face(h, f).start()
 
-    for h in range(2):
-        c = cols[h]
+    def direction_part(h):
+        c, hw = cols[h], widths[h]
+        first = CUTS[h] * part_w
         for f in (4, 5, 2, 3, 0, 1):
             rows = pl.ds(f * face, face)
             image_face(h, f ^ 1).wait_recv()
             live = iota((face, hw), 0) < fl_ref[f]
-            p = jnp.where(
-                live, 0.5 * (img_v[rows, c] + rx1[f, :, c]) + beta[:, h * hw : (h + 1) * hw] * pp_v[rows, c], 0.0
-            )
+            p = 0.5 * (img_v[rows, c] + rx1[f, :, c]) + beta[:, first : first + hw] * pp_v[rows, c]
+            p = jnp.where(live, p, 0.0)
             p_v[rows, c] = p
             ph, plo = split(p)
             wh_v[rows, c] = ph
             wl_v[rows, c] = plo
 
-        def schur_block(f, acc):
+    done = 0
+    for first, last in GROUPS:
+        while done < chunks and CUTS[done + 1] <= last:
+            direction_part(done)
+            done += 1
+        c = pl.ds(first * part_w, (last - first) * part_w)
+
+        def schur_block(f, acc, c=c):
             rows = pl.ds(pl.multiple_of(f * face, face), face)
             y = mm3(s_v[rows, :], wh_v[:, c], wl_v[:, c])
             simg_v[rows, c] = y
             return acc + jnp.sum(p_v[rows, c] * y, axis=0, keepdims=True)
 
-        ar_src[1, :, c] = lax.fori_loop(0, 6, schur_block, jnp.zeros((1, hw), F32))
+        ar_src[1, :, c] = lax.fori_loop(
+            0, 6, schur_block, jnp.zeros((1, (last - first) * part_w), F32)
+        )
     dir_out = pltpu.make_async_copy(p_v, dir_hbm, o_sem.at[0])
     dir_out.start()
     reduce_start(1)
     for f in range(6):
         schur_face(f).start()
     reduce_middle(1)
-    alpha = rho_now / (norm_scale * (2.0 * reduce_end(1)))
-    small_ref[1] = alpha
-
-    total = jnp.zeros((1, nr), F32)
     for f in (4, 5, 2, 3, 0, 1):
         rows = pl.ds(f * face, face)
         schur_face(f ^ 1).wait_recv()
         live = iota((face, nr), 0) < fl_ref[f]
-        q = r_v[rows, :] - alpha * jnp.where(live, simg_v[rows, :] + rx2[f], 0.0)
+        nloc_v[rows, :] = jnp.where(live, simg_v[rows, :] + rx2[f], 0.0)
+    alpha = rho_now / (norm_scale * (2.0 * reduce_end(1)))
+    small_ref[1] = alpha
+
+    total = jnp.zeros((1, nr), F32)
+    for f in range(6):
+        rows = pl.ds(f * face, face)
+        q = r_v[rows, :] - alpha * nloc_v[rows, :]
         nloc_v[rows, :] = q
         total = total + jnp.sum(q * q, axis=0, keepdims=True)
     ar_src[2] = total
@@ -446,14 +441,14 @@
 
     left(rows_out.at[most], row_s.at[0])
     for way in range(2):
-        for h in range(2):
-            left(out_buf.at[h, most], x_s.at[way, h])
+        for h in range(chunks):
+            left(out_buf.at[most, :, cols[h]], x_s.at[way, h])
     for k in range(3):
         left(ar_a.at[k, most], ara_s.at[k])
         left(ar_b.at[k, pl.ds(0, n_depth - 1)], arb_s.at[k])
     for f in range(6):
-        image_face(0, f).wait_send()
-        image_face(1, f).wait_send()
+        for h in range(chunks):
+            image_face(h, f).wait_send()
         schur_face(f).wait_send()
 
 
@@ -501,6 +496,7 @@
     vm, sem = pltpu.VMEM, pltpu.SemaphoreType.DMA
     whole = pl.BlockSpec(memory_space=pltpu.VMEM)
     far = pl.BlockSpec(memory_space=pl.ANY)
+    hbm = pl.BlockSpec(memory_space=pltpu.HBM)
     big = jax.ShapeDtypeStruct((nb, nr), F32)
     small = jax.ShapeDtypeStruct((1, nr), F32)
     scratch = [
@@ -522,10 +518,10 @@
         vm((sizes[0], sizes[1] * STRIDE, co), BF16),
         vm((owners, 1, 4 * STRIDE), F32),
         vm((owners, 1, 4 * STRIDE), F32),
-        vm((2, owners, CAP, nr // 2), F32),
-        vm((2, owners, STRIDE, nr // 2), F32),
-        vm((2, owners, STRIDE, nr // 2), F32),
-        vm((2, owners, CAP, nr // 2), F32),
+        vm((owners, CAP, nr), F32),
+        vm((owners, STRIDE, nr), F32),
+        vm((owners, STRIDE, nr), F32),
+        vm((owners, CAP, nr), F32),
         vm((nc, nr), F32),
         vm((nb, nr), F32),
         vm((nb, nr), F32),
@@ -540,20 +536,20 @@
         sem((6,)),
         sem((1,)),
         sem((1,)),
-        sem((2, 2)),
-        sem((2, 2)),
+        sem((2, len(CUTS) - 1)),
+        sem((2, len(CUTS) - 1)),
         sem((3,)),
         sem((3,)),
         sem((3,)),
         sem((3,)),
-        sem((3, 6)),
-        sem((3, 6)),
+        sem((len(CUTS), 6)),
+        sem((len(CUTS), 6)),
         sem((2,)),
     ]
     q, p, totals = pl.pallas_call(
         functools.partial(step_kernel, sizes, norm_scale),
         out_shape=(big, big, jax.ShapeDtypeStruct((3, 1, nr), F32)),
-        in_specs=[pl.BlockSpec(memory_space=pltpu.SMEM), whole, whole, whole] + [far] * 6,
+        in_specs=[pl.BlockSpec(memory_space=pltpu.SMEM), whole, whole, whole] + [hbm] * 6,
         out_specs=(far, far, whole),
         scratch_shapes=scratch,
         compiler_params=pltpu.CompilerParams(

time: 121 us -> 119 us (0.983)
  Pallas kernels: 120 us -> 118 us
    pallas_call x1, Pallas kernels: 116 us -> 114 us  [shards(): pl.pallas_call(functools.partial(step_kernel, sizes, norm_scale), out_sha...]
where the time goes in v3:
time: 119 us
  Pallas kernels  118 us (99%)
    pallas_call x1, Pallas kernels, shards(): pl.pallas_call(functools.partial(step_kernel, sizes, norm_scale), out_sha...  114 us
    pallas_call x1, Pallas kernels, shards(): pl.pallas_call(pass_kernel, out_shape=(big, big, small, small, small), in...  4.06 us

profile of v3, /device:TPU:1, one launch (start us, length us, event | category | flops | bytes accessed | tf_op | source)
XLA Modules:
  0.0 119.0 jit_solution(14163919175953858426)
XLA Ops:
  0.6 114.3 %shard_map.137 = (f32[768,512]{1,0:T(8,128)}, f32[768,512]{1,0:T(8,128)}, f32[3,1,512]{2,1,0:T(1,128)}) custom-call(s32[6]{0:T(128)} %bitcast.24, s32[1,256]{1,0:T(1,128)} %bitcast.22, s32[1,256]{1,0:T(1,128)} %bitcast.23, f32[1,512]{1,0:T(1,128)} %bitcast.21, f32[768,512]{1,0:T(8,128)} %bitcast.17, f32[768,512]{1,0:T(8,128)} %bitcast.18, ...), custom_call_target="tpu_custom_call" | custom-call | tf_op jit(solution)/shard_map/pallas_call | solution.py:549
  114.9 4.1 %shard_map.138 = (f32[768,512]{1,0:T(8,128)}, f32[768,512]{1,0:T(8,128)}, f32[1,512]{1,0:T(1,128)}, f32[1,512]{1,0:T(1,128)}, f32[1,512]{1,0:T(1,128)}) custom-call(f32[768,512]{1,0:T(8,128)} %get-tuple-element.13.q_hbm, f32[768,512]{1,0:T(8,128)} %get-tuple-element.14.p_hbm, f32[3,1,512]{2,1,0:T(1,128)} %get-tuple-element.15.small), custom_call_target="tpu_custom_call" | custom-call | tf_op jit(solution)/shard_map/pallas_call | solution.py:570

commit v4 on v3

--- a/solution.py
+++ b/solution.py
@@ -327,13 +327,6 @@
             tiles = mm(pick, th_v[:, c]) + mm(pick, tl_v[:, c])
             ans_buf[pl.ds(tb * n_lat, n_lat), :, c] = tiles.reshape(n_lat, STRIDE, hw)
             tile_sends(ans_of, ret_of, 1, h, db)
-    reduce_middle(0)
-    rho_now = norm_scale * reduce_end(0)
-    small_ref[0] = rho_now
-    beta = rho_now / prho_ref[...]
-    loads[4].wait()
-    loads[5].wait()
-
     def face_copy(src, rx, f, c, ssem, rsem):
         step = 1 if f % 2 == 1 else -1
         axis = f // 2
@@ -374,6 +367,14 @@
             rows = pl.ds(f * face, face)
             img_v[rows, c] = nloc_v[rows, c] + mm3(phi_v[rows, :], ch, cl)
             image_face(h, f).start()
+        if h == 0:
+            reduce_middle(0)
+
+    rho_now = norm_scale * reduce_end(0)
+    small_ref[0] = rho_now
+    beta = rho_now / prho_ref[...]
+    loads[4].wait()
+    loads[5].wait()
 
     def direction_part(h):
         c, hw = cols[h], widths[h]
@@ -452,25 +453,18 @@
         schur_face(f).wait_send()
 
 
-def pass_kernel(q_hbm, p_hbm, small, nr_hbm, dir_hbm, rho_ref, alpha_ref, norm_ref, q_v, p_v, sems):
-    parts = 4
-    rows = q_v.shape[0] // parts
-    ins, outs = [], []
-    for k, (src, mid, dst) in enumerate(((p_hbm, p_v, dir_hbm), (q_hbm, q_v, nr_hbm))):
-        for i in range(parts):
-            at = pl.ds(i * rows, rows)
-            ins.append(pltpu.make_async_copy(src.at[at], mid.at[at], sems.at[0, k, i]))
-            outs.append(pltpu.make_async_copy(mid.at[at], dst.at[at], sems.at[1, k, i]))
-    for one in ins:
+def pass_kernel(q_ref, p_ref, small, nr_hbm, dir_hbm, rho_ref, alpha_ref, norm_ref, sems):
+    moves = [
+        pltpu.make_async_copy(q_ref, nr_hbm, sems.at[0]),
+        pltpu.make_async_copy(p_ref, dir_hbm, sems.at[1]),
+    ]
+    for one in moves:
         one.start()
     rho_ref[...] = small[0]
     alpha_ref[...] = small[1]
     norm_ref[...] = small[2]
-    for got, out in zip(ins, outs):
-        got.wait()
-        out.start()
-    for out in outs:
-        out.wait()
+    for one in moves:
+        one.wait()
 
 
 def shards(
@@ -553,26 +547,27 @@
         out_specs=(far, far, whole),
         scratch_shapes=scratch,
         compiler_params=pltpu.CompilerParams(
-            collective_id=0, has_side_effects=True, vmem_limit_bytes=60 * 1024 * 1024
+            collective_id=0, has_side_effects=True, vmem_limit_bytes=44 * 1024 * 1024
         ),
     )(
-        face_len.reshape(6),
-        prim_owner.reshape(1, nc),
-        coarse_row.reshape(1, nc),
-        prev_rho.reshape(1, nr),
-        residual.reshape(nb, nr),
-        prev_direction.reshape(nb, nr),
-        schur.reshape(nb, nb),
-        neumann.reshape(nb, nb),
-        coarse_basis.reshape(nb, nc),
-        coarse_inverse.reshape(co, co),
+        pltpu.with_memory_space_constraint(face_len.reshape(6), pltpu.HBM),
+        pltpu.with_memory_space_constraint(prim_owner.reshape(1, nc), pltpu.HBM),
+        pltpu.with_memory_space_constraint(coarse_row.reshape(1, nc), pltpu.HBM),
+        pltpu.with_memory_space_constraint(prev_rho.reshape(1, nr), pltpu.HBM),
+        pltpu.with_memory_space_constraint(residual.reshape(nb, nr), pltpu.HBM),
+        pltpu.with_memory_space_constraint(prev_direction.reshape(nb, nr), pltpu.HBM),
+        pltpu.with_memory_space_constraint(schur.reshape(nb, nb), pltpu.HBM),
+        pltpu.with_memory_space_constraint(neumann.reshape(nb, nb), pltpu.HBM),
+        pltpu.with_memory_space_constraint(coarse_basis.reshape(nb, nc), pltpu.HBM),
+        pltpu.with_memory_space_constraint(coarse_inverse.reshape(co, co), pltpu.HBM),
     )
     new_residual, direction, rho_now, step_alpha, res_norm = pl.pallas_call(
         pass_kernel,
         out_shape=(big, big, small, small, small),
         in_specs=[far, far, whole],
-        out_specs=(far, far, whole, whole, whole),
-        scratch_shapes=[vm((nb, nr), F32), vm((nb, nr), F32), sem((2, 2, 4))],
+        out_specs=(hbm, hbm, whole, whole, whole),
+        scratch_shapes=[sem((2,))],
+        compiler_params=pltpu.CompilerParams(vmem_limit_bytes=4 * 1024 * 1024),
     )(q, p, totals)
     out_shape = (1, 1, 1, nb, nr)
     return (

time: 119 us -> 117 us (0.983)
  Pallas kernels: 118 us -> 116 us
    pallas_call x1, Pallas kernels: 4.06 us -> 2.27 us  [shards(): pl.pallas_call(pass_kernel, out_shape=(big, big, small, small, small), in...]
where the time goes in v4:
time: 117 us
  Pallas kernels  116 us (99%)
    pallas_call x1, Pallas kernels, shards(): pl.pallas_call(functools.partial(step_kernel, sizes, norm_scale), out_sha...  114 us

profile of v4, /device:TPU:1, one launch (start us, length us, event | category | flops | bytes accessed | tf_op | source)
XLA Modules:
  0.0 116.7 jit_solution(4425089055732146658)
XLA Ops:
  0.6 113.8 %shard_map.137 = (f32[768,512]{1,0:T(8,128)S(1)}, f32[768,512]{1,0:T(8,128)S(1)}, f32[3,1,512]{2,1,0:T(1,128)S(1)}) custom-call(s32[6]{0:T(128)} %bitcast.24, s32[1,256]{1,0:T(1,128)} %bitcast.22, s32[1,256]{1,0:T(1,128)} %bitcast.23, f32[1,512]{1,0:T(1,128)} %bitcast.21, f32[768,512]{1,0:T(8,128)} %bitcast.17, f32[768,512]{1,0:T(8,128)} %bitcast.18, ...), custom_call_target="tpu_custom_call" | custom-call | tf_op jit(solution)/shard_map/pallas_call | solution.py:543
  114.4 2.3 %shard_map.138 = (f32[768,512]{1,0:T(8,128)}, f32[768,512]{1,0:T(8,128)}, f32[1,512]{1,0:T(1,128)}, f32[1,512]{1,0:T(1,128)}, f32[1,512]{1,0:T(1,128)}) custom-call(f32[768,512]{1,0:T(8,128)S(1)} %get-tuple-element.13.q_ref, f32[768,512]{1,0:T(8,128)S(1)} %get-tuple-element.14.p_ref, f32[3,1,512]{2,1,0:T(1,128)S(1)} %get-tuple-element.15.small), custom_call_target="tpu_custom_call" | custom-call | tf_op jit(solution)/shard_map/pallas_call | solution.py:564
